TPU v7x, 256 devices: a whole 4x4x8 slice. The times are simulated.
256 devices in a mesh: pb: 32 (over y, z_lo, core), ka: 8 (over z_hi, x).
Axes of the slice: x: 4, y: 4, z: 8 (z_hi: 2, z_lo: 4; z = z_hi * 4 + z_lo), core: 2. Of those that a mesh axis runs over, the one named last changes fastest.
Arguments:
- queries: bfloat16 [32768, 1024], P(('pb', 'ka')), may hold values from -6 to 6
- key_vectors: bfloat16 [32768, 128], P(('pb', 'ka')), may hold values from -6 to 6
- value_vectors: bfloat16 [32768, 128], P(('pb', 'ka')), may hold values from -6 to 6
- out_grad: bfloat16 [32768, 1024], P(('pb', 'ka')), may hold values from -6 to 6
- rand_blocks: int32 [512, 3], P('pb'), may hold values from 0 to 511
- global_blocks: int32 [2], replicated, may hold values from 0 to 511
Outputs:
- attended: bfloat16 [32768, 1024], P(('pb', 'ka'))
- query_grad: bfloat16 [32768, 1024], P(('pb', 'ka'))
- key_grad: bfloat16 [32768, 128], P(('pb', 'ka'))
- value_grad: bfloat16 [32768, 128], P(('pb', 'ka'))
All inputs are finite; a program needn't handle non-finite values.
Results may differ from a plain program's by a relative error of at most 0.024.
Values may be sent and summed in bfloat16 or wider, within the bound.
A program may use at most 128 MiB of HBM per device.

v0:
```python
import math

import jax
import jax.numpy as jnp
from jax import lax
from jax.sharding import PartitionSpec as P

BLOCK = 64


NEG_FILL = -1e30


def candidates(block_ids, global_blocks, rand_rows, block_total):
    nearby = jnp.stack([block_ids - 1, block_ids, block_ids + 1], axis=1)
    global_cols = jnp.broadcast_to(
        global_blocks[None, :], (block_ids.shape[0], global_blocks.shape[0])
    )
    cand = jnp.concatenate([nearby, global_cols, rand_rows], axis=1)
    in_range = (cand >= 0) & (cand < block_total)
    slot_count = cand.shape[1]
    equal_pairs = cand[:, :, None] == cand[:, None, :]
    earlier_slot = jnp.arange(slot_count)[None, :, None] > jnp.arange(slot_count)[None, None, :]
    repeated = jnp.any(equal_pairs & earlier_slot, axis=2)
    valid_slots = in_range & jnp.logical_not(repeated)
    safe_slots = jnp.clip(cand, 0, block_total - 1)
    return (safe_slots, valid_slots)


def body(queries, key_vectors, value_vectors, out_grad, rand_blocks, global_blocks):
    ka_size = lax.axis_size("ka")
    pb_size = lax.axis_size("pb")
    row_index = lax.axis_index("pb")
    col_index = lax.axis_index("ka")
    tok_rows = queries.shape[0]
    head_dim = key_vectors.shape[1]
    head_count = queries.shape[1] // head_dim
    per_shard = tok_rows // BLOCK
    query_blocks = per_shard * ka_size
    key_blocks = per_shard * pb_size
    block_total = query_blocks * pb_size
    score_scale = 1.0 / math.sqrt(head_dim)
    glob_count = global_blocks.shape[0]
    pair_batch = 16
    block_heads = BLOCK * head_count
    q_tile, d_tile = (
        lax.all_gather(queries, "ka", axis=0, tiled=True),
        lax.all_gather(out_grad, "ka", axis=0, tiled=True),
    )
    k_tile, v_tile = (
        lax.all_gather(key_vectors, "pb", axis=0, tiled=True),
        lax.all_gather(value_vectors, "pb", axis=0, tiled=True),
    )
    q_grid = q_tile.reshape(query_blocks, block_heads, head_dim)
    d_grid = d_tile.reshape(query_blocks, block_heads, head_dim)
    k_grid = k_tile.reshape(key_blocks, BLOCK, head_dim)
    v_grid = v_tile.reshape(key_blocks, BLOCK, head_dim)
    block_ids = row_index * query_blocks + jnp.arange(query_blocks, dtype=jnp.int32)
    safe_slots, valid_slots = candidates(block_ids, global_blocks, rand_blocks, block_total)
    slot_count = safe_slots.shape[1]
    shard_ids = safe_slots // per_shard
    owned_slots = shard_ids % ka_size == col_index
    local_key = shard_ids // ka_size * per_shard + safe_slots % per_shard
    is_global = jnp.any(block_ids[:, None] == global_blocks[None, :], axis=1)
    slot_flag = valid_slots & owned_slots & jnp.logical_not(is_global)[:, None]
    dense_flag = jnp.broadcast_to(is_global[:, None], (query_blocks, key_blocks))
    dense_targets = jnp.broadcast_to(
        jnp.arange(key_blocks, dtype=jnp.int32)[None, :], (query_blocks, key_blocks)
    )
    pair_flags = jnp.concatenate([slot_flag, dense_flag], axis=1)
    pair_targets = jnp.concatenate([local_key, dense_targets], axis=1)
    capacity = query_blocks * slot_count + glob_count * key_blocks
    capacity = -(-capacity // pair_batch) * pair_batch
    flat_flags = pair_flags.reshape(-1)
    flat_targets = pair_targets.reshape(-1)
    flat_owner = jnp.broadcast_to(
        jnp.arange(query_blocks, dtype=jnp.int32)[:, None], pair_flags.shape
    ).reshape(-1)
    pair_order = jnp.cumsum(flat_flags.astype(jnp.int32)) - 1
    where_to = jnp.where(flat_flags, pair_order, capacity)
    pair_row = jnp.zeros((capacity,), jnp.int32).at[where_to].set(flat_owner, mode="drop")
    pair_key = jnp.zeros((capacity,), jnp.int32).at[where_to].set(flat_targets, mode="drop")
    per_row = jnp.sum(pair_flags.astype(jnp.int32), axis=1)
    row_bounds = jnp.concatenate([jnp.zeros((1,), jnp.int32), jnp.cumsum(per_row)])
    pair_total = row_bounds[query_blocks]

    def sweep_pairs(low_pair, high_pair, visitor, carry_in):

        def advance(batch_index, carry_now):
            first_pair = batch_index * pair_batch
            pair_slots = first_pair + jnp.arange(pair_batch, dtype=jnp.int32)
            live_pairs = (pair_slots >= low_pair) & (pair_slots < high_pair)
            row_ids = lax.dynamic_slice_in_dim(pair_row, first_pair, pair_batch)
            key_ids = lax.dynamic_slice_in_dim(pair_key, first_pair, pair_batch)
            return visitor(carry_now, row_ids, key_ids, live_pairs)

        return lax.fori_loop(
            low_pair // pair_batch, (high_pair + pair_batch - 1) // pair_batch, advance, carry_in
        )

    def scores(row_ids, key_ids, live_pairs):
        q_sel = q_grid[row_ids]
        k_sel = k_grid[key_ids]
        raw_scores = (
            jnp.einsum("pre,pke->prk", q_sel, k_sel, preferred_element_type=jnp.float32)
            * score_scale
        )
        return (q_sel, k_sel, jnp.where(live_pairs[:, None, None], raw_scores, NEG_FILL))

    empty_max = jnp.full((query_blocks, block_heads), NEG_FILL, jnp.float32)
    empty_sum = jnp.zeros((query_blocks, block_heads), jnp.float32)

    def visit_max(carry_now, row_ids, key_ids, live_pairs):
        raw_scores = scores(row_ids, key_ids, live_pairs)[2]
        return carry_now.at[row_ids].max(jnp.max(raw_scores, axis=2))

    row_max = lax.pmax(sweep_pairs(0, pair_total, visit_max, empty_max), "ka")

    def visit_sum(carry_now, row_ids, key_ids, live_pairs):
        raw_scores = scores(row_ids, key_ids, live_pairs)[2]
        return carry_now.at[row_ids].add(
            jnp.sum(jnp.exp(raw_scores - row_max[row_ids][:, :, None]), axis=2)
        )

    row_sum = lax.psum(sweep_pairs(0, pair_total, visit_sum, empty_sum), "ka")

    def weights_of(raw_scores, row_ids, live_pairs):
        weights = jnp.exp(raw_scores - row_max[row_ids][:, :, None]) / row_sum[row_ids][:, :, None]
        return jnp.where(live_pairs[:, None, None], weights, 0.0)

    first_block = jnp.int32(0) // BLOCK
    block_span = lax.axis_size("ka") * tok_rows // BLOCK

    def visit_out(totals, row_ids, key_ids, live_pairs):
        raw_scores = scores(row_ids, key_ids, live_pairs)[2]
        weights_bf = weights_of(raw_scores, row_ids, live_pairs).astype(jnp.bfloat16)
        partial_value = jnp.einsum(
            "prk,pke->pre", weights_bf, v_grid[key_ids], preferred_element_type=jnp.float32
        )
        target = jnp.clip(row_ids, 0, block_span - 1)
        return totals.at[target].add(partial_value)

    totals = sweep_pairs(
        row_bounds[first_block],
        row_bounds[first_block + block_span],
        visit_out,
        jnp.zeros((block_span, block_heads, head_dim), jnp.float32),
    )
    out_rows = lax.psum_scatter(
        totals.reshape(lax.axis_size("ka") * tok_rows, head_count * head_dim),
        "ka",
        scatter_dimension=0,
        tiled=True,
    )
    attended = out_rows.astype(jnp.bfloat16)
    own_dots = jnp.sum(
        (out_grad.astype(jnp.float32) * attended.astype(jnp.float32)).reshape(
            tok_rows, head_count, head_dim
        ),
        axis=2,
    )
    dot_tile = lax.all_gather(own_dots, "ka", axis=0, tiled=True).reshape(query_blocks, block_heads)

    def visit_grads(carry_now, row_ids, key_ids, live_pairs):
        query_acc, key_acc, value_acc = carry_now
        q_sel, k_sel, raw_scores = scores(row_ids, key_ids, live_pairs)
        weights = weights_of(raw_scores, row_ids, live_pairs)
        d_sel = d_grid[row_ids]
        prob_grad = jnp.einsum(
            "pre,pke->prk", d_sel, v_grid[key_ids], preferred_element_type=jnp.float32
        )
        score_grad = (weights * (prob_grad - dot_tile[row_ids][:, :, None])).astype(jnp.bfloat16)
        query_acc = query_acc.at[row_ids].add(
            jnp.einsum("prk,pke->pre", score_grad, k_sel, preferred_element_type=jnp.float32)
            * score_scale
        )
        key_acc = key_acc.at[key_ids].add(
            jnp.einsum("prk,pre->pke", score_grad, q_sel, preferred_element_type=jnp.float32)
            * score_scale
        )
        value_acc = value_acc.at[key_ids].add(
            jnp.einsum(
                "prk,pre->pke",
                weights.astype(jnp.bfloat16),
                d_sel,
                preferred_element_type=jnp.float32,
            )
        )
        return (query_acc, key_acc, value_acc)

    zero_queries = jnp.zeros((query_blocks, block_heads, head_dim), jnp.float32)
    zero_keys = jnp.zeros((key_blocks, BLOCK, head_dim), jnp.float32)
    query_acc, key_acc, value_acc = sweep_pairs(
        0, pair_total, visit_grads, (zero_queries, zero_keys, zero_keys)
    )
    key_sum, value_sum = (
        lax.psum_scatter(
            key_acc.reshape(key_blocks * BLOCK, head_dim), "pb", scatter_dimension=0, tiled=True
        ),
        lax.psum_scatter(
            value_acc.reshape(key_blocks * BLOCK, head_dim), "pb", scatter_dimension=0, tiled=True
        ),
    )
    dq_rows = lax.psum_scatter(
        query_acc.reshape(query_blocks * BLOCK, head_count * head_dim),
        "ka",
        scatter_dimension=0,
        tiled=True,
    )
    return (
        attended,
        dq_rows.astype(jnp.bfloat16),
        key_sum.astype(jnp.bfloat16),
        value_sum.astype(jnp.bfloat16),
    )


def solution(mesh):
    placed = (
        P(("pb", "ka"), None),
        P(("pb", "ka"), None),
        P(("pb", "ka"), None),
        P(("pb", "ka"), None),
        P("pb", None),
        P(),
    )
    return jax.shard_map(
        body,
        mesh=mesh,
        in_specs=placed,
        out_specs=(
            P(("pb", "ka"), None),
            P(("pb", "ka"), None),
            P(("pb", "ka"), None),
            P(("pb", "ka"), None),
        ),
        check_vma=False,
    )
```

profile of v0, /device:TPU:2, one launch (start us, length us, event | category | flops | bytes accessed | tf_op | source)
XLA Modules:
  0.0 1294.6 jit_solution(18129944820504423100)
XLA Ops:
  7.2 0.7 all-gather.5.cloned.1.call-update
  7.9 0.7 all-gather.7.cloned.1.call-update
  8.7 0.7 all-gather.9.cloned.1.call-update
  10.1 0.7 compare_reduce_fusion
  10.8 0.7 broadcast_in_dim.159
  11.5 0.7 concatenate.10
  12.5 0.7 convert_reduce_fusion
  15.1 6.4 scatter_custom_fusion.7
  21.6 6.4 scatter_custom_fusion.6
  28.0 61.2 %all-gather.5.cloned.1.call-done = bf16[1024,1024]{1,0:T(8,128)(2,1)} async-done(((bf16[128,1024]{1,0:T(8,128)(2,1)}), bf16[1024,1024]{1,0:T(8,128)(2,1)}) %all-gather.5.cloned.1.call-update) | async-done | bytes 2097168 | tf_op jit(solution)/shard_map/all_gather | solution.py:47
  89.2 2.8 reshape.188
  92.0 53.8 %all-gather.7.cloned.1.call-done = bf16[4096,128]{1,0:T(8,128)(2,1)} async-done(((bf16[128,128]{1,0:T(8,128)(2,1)}), bf16[4096,128]{1,0:T(8,128)(2,1)}) %all-gather.7.cloned.1.call-update) | async-done | bytes 1048592 | tf_op jit(solution)/shard_map/all_gather | solution.py:51
  145.8 8.0 while.45
  145.8 0.7 compare_and_fusion.8
  146.6 1.8 gather_fusion.1
  148.4 2.2 gather_fusion
  150.6 2.5 select_reduce_fusion.2
  153.0 0.7 scatter_fusion
  153.8 48.7 %pmax.7 = f32[16,512]{1,0:T(8,128)S(1)} all-reduce(f32[16,512]{1,0:T(8,128)S(1)} %get-tuple-element.272), channel_id=1, replica_groups=mesh['pb'=32,'ka'=8] {'ka'}, use_global_device_ids=true, to_apply=%region_11.12 | all-reduce | flops 8192 | bytes 65536 | tf_op jit(solution)/shard_map/pmax | solution.py:117
  202.5 8.6 while.46
  202.5 0.7 compare_and_fusion.9
  203.9 1.8 gather_fusion.3
  205.7 2.2 gather_fusion.2
  207.9 2.5 exponential_reduce_fusion.2
  210.4 0.7 scatter_fusion.1
  211.1 55.7 %psum.7 = f32[16,512]{1,0:T(8,128)S(1)} all-reduce(f32[16,512]{1,0:T(8,128)S(1)} %get-tuple-element.273), channel_id=1, replica_groups=mesh['pb'=32,'ka'=8] {'ka'}, use_global_device_ids=true, to_apply=%region_16.17 | all-reduce | flops 8192 | bytes 65536 | tf_op jit(solution)/shard_map/psum | solution.py:125
  266.8 2.4 broadcast.237.clone
  269.2 21.9 %while.47 = (s32[]{:T(128)}, f32[16,512,128]{2,1,0:T(8,128)}, s32[]{:T(128)}, s32[256]{0:T(256)S(1)}, s32[]{:T(128)}, /*index=5*/bf16[16,512,128]{2,1,0:T(8,128)...) while((s32[]{:T(128)}, f32[16,512,128]{2,1,0:T(8,128)}, ...), condition=%wide.region_19.20_spmd, body=%wide.region_17.19_spmd.sunk | while | flops 272632032 | bytes 24847400 | solution.py:97
  271.2 1.8 gather_fusion.7
  273.0 1.8 gather_fusion.5
  274.8 2.2 gather_fusion.6
  277.0 5.1 fusion.69
  282.1 9.1 scatter_fusion.2
  291.2 4.9 reshape.192
  296.1 4.2 reshape.193
  300.4 295.7 %reduce-scatter.5.cloned.1.call-done = f32[128,1024]{1,0:T(8,128)} async-done(((f32[1024,1024]{1,0:T(8,128)}), f32[128,1024]{1,0:T(8,128)}) %reduce-scatter.5.cloned.1.call-update) | async-done | bytes 524304 | tf_op jit(solution)/shard_map/reduce_scatter | solution.py:149
  596.1 1.8 multiply_bitcast_fusion
  598.3 40.2 %all_gather.19 = f32[1024,8]{1,0:T(8,128)S(1)} all-gather(f32[128,8]{1,0:T(8,128)S(1)} %reduce_sum.17), channel_id=1, replica_groups=mesh['pb'=32,'ka'=8] {'ka'}, dimensions={0}, use_global_device_ids=true | all-gather | bytes 36864 | tf_op jit(solution)/shard_map/all_gather | solution.py:162
  638.7 1.6 broadcast_in_dim.166.clone
  640.3 1.6 broadcast_in_dim.166
  641.9 2.4 broadcast.237
  644.3 37.2 %while.48 = (s32[]{:T(128)}, f32[16,512,128]{2,1,0:T(8,128)}, f32[64,64,128]{2,1,0:T(8,128)}, f32[64,64,128]{2,1,0:T(8,128)}, s32[]{:T(128)}, /*index=5*/s32[256...) while((s32[]{:T(128)}, f32[16,512,128]{2,1,0:T(8,128)}, ...), condition=%wide.region_26.27_spmd, body=%wide.region_22.26_spmd.sunk | while | flops 678299776 | bytes 67151200 | solution.py:97
  644.3 0.7 compare_and_fusion.11
  646.8 1.8 gather_fusion.11
  648.6 2.5 gather_fusion.15
  651.1 3.7 gather_fusion.14
  654.8 2.2 gather_fusion.10
  657.0 2.6 divide_select_fusion.2
  659.6 1.3 fusion.80
  660.9 0.9 multiply_convert_fusion.2
  661.7 0.7 copy-done.1
  662.5 1.3 convolution_multiply_fusion.5
  663.8 3.0 scatter_fusion.4
  666.8 3.0 scatter_fusion.5
  669.7 2.7 convolution_multiply_fusion.4
  672.4 9.1 scatter_fusion.3
  681.6 0.7 reduce-scatter.9.cloned.1.call-update
  682.3 4.9 reshape.196
  687.2 327.0 %reduce-scatter.11.cloned.1.call-done = f32[128,128]{1,0:T(8,128)} async-done(((f32[4096,128]{1,0:T(8,128)}), f32[128,128]{1,0:T(8,128)}) %reduce-scatter.11.cloned.1.call-update) | async-done | bytes 65552 | tf_op jit(solution)/shard_map/reduce_scatter | solution.py:200
  1014.2 1.5 convert_element_type.47
  1015.7 146.4 %reduce-scatter.9.cloned.1.call-done = f32[128,128]{1,0:T(8,128)} async-done(((f32[4096,128]{1,0:T(8,128)}), f32[128,128]{1,0:T(8,128)}) %reduce-scatter.9.cloned.1.call-update) | async-done | bytes 65552 | tf_op jit(solution)/shard_map/reduce_scatter | solution.py:197
  1162.1 1.5 convert_element_type.46
  1163.5 122.5 %reduce-scatter.7.cloned.1.call-done = f32[128,1024]{1,0:T(8,128)} async-done(((f32[1024,1024]{1,0:T(8,128)}), f32[128,1024]{1,0:T(8,128)}) %reduce-scatter.7.cloned.1.call-update) | async-done | bytes 524304 | tf_op jit(solution)/shard_map/reduce_scatter | solution.py:204
  1286.0 1.8 convert_element_type.45
  (70 shorter events, 7.5 us)
Async XLA Ops:
  7.2 82.0 %all-gather.5.cloned.1.call-start = ((), (), s32[]{:S(2)}) async-start(), calls=%async_computation.4 | async-start | bytes 2359296 | tf_op jit(solution)/shard_map/all_gather | solution.py:47
  7.9 137.9 %all-gather.7.cloned.1.call-start = ((), (), s32[]{:S(2)}) async-start(), calls=%async_computation.5 | async-start | bytes 1081344 | tf_op jit(solution)/shard_map/all_gather | solution.py:51
  8.6 258.2 %all-gather.9.cloned.1.call-start = ((), (), s32[]{:S(2)}) async-start(), calls=%async_computation.6 | async-start | bytes 1081344 | tf_op jit(solution)/shard_map/all_gather | solution.py:52
  9.4 286.8 %all-gather.11.cloned.1.call-start = ((), (), s32[]{:S(2)}) async-start(), calls=%async_computation.8 | async-start | bytes 2359296 | tf_op jit(solution)/shard_map/all_gather | solution.py:48
  10.0 586.2 %reduce-scatter.5.cloned.1.call-start = ((), (), s32[]{:S(2)}) async-start(), calls=%async_computation.7 | async-start | bytes 4718592 | tf_op jit(solution)/shard_map/reduce_scatter | solution.py:149
  296.1 718.2 %reduce-scatter.11.cloned.1.call-start = ((), (), s32[]{:S(2)}) async-start(), calls=%async_computation.11 | async-start | bytes 2162688 | tf_op jit(solution)/shard_map/reduce_scatter | solution.py:200
  296.1 300.0 %copy-start.3 = (bf16[128,1024]{1,0:T(8,128)(2,1)S(1)}, bf16[128,1024]{1,0:T(8,128)(2,1)}, u32[]{:S(2)}) copy-start(bf16[128,1024]{1,0:T(8,128)(2,1)} %param.17) | copy-start | bytes 786436
  657.0 2.6 copy-start
  659.6 1.3 copy-start.2
  660.9 1.6 copy-start.1
  681.5 480.5 %reduce-scatter.9.cloned.1.call-start = ((), (), s32[]{:S(2)}) async-start(), calls=%async_computation.10 | async-start | bytes 2162688 | tf_op jit(solution)/shard_map/reduce_scatter | solution.py:197
  682.3 603.7 %reduce-scatter.7.cloned.1.call-start = ((), (), s32[]{:S(2)}) async-start(), calls=%async_computation.9 | async-start | bytes 4718592 | tf_op jit(solution)/shard_map/reduce_scatter | solution.py:204
Sparse Core Ops, SparseCore 0:
  10.6 78.5 all-gather.4
  91.1 54.7 all-gather.6
  147.7 57.5 all-gather.8
  207.8 74.8 all-gather.10
  296.2 299.8 reduce-scatter.4
  681.7 332.5 reduce-scatter.10
  1016.7 145.2 reduce-scatter.8
  1166.2 119.7 reduce-scatter.6
where the time goes:
time: 1300 us; the launch traced here: 1290 us
  waiting for transfers between devices  1010 us (78%)
  blocking collectives  145 us (11%)
  local copies, waits for them, and re-layouts  68.5 us (5%)
  other arithmetic  37.5 us (3%)
  matrix products  18.8 us (1%)
  between operations  15 us (1%)
    reduce_scatter x1, waiting for transfers between devices, body(): lax.psum_scatter(value_acc.reshape(key_blocks * BLOCK, head_dim), 'pb', s...  327 us
    reduce_scatter x1, waiting for transfers between devices, body(): lax.psum_scatter(totals.reshape(lax.axis_size('ka') * tok_rows, head_coun...  296 us
    reduce_scatter x1, waiting for transfers between devices, body(): lax.psum_scatter(key_acc.reshape(key_blocks * BLOCK, head_dim), 'pb', sca...  146 us
    reduce_scatter x1, waiting for transfers between devices, body(): lax.psum_scatter(query_acc.reshape(query_blocks * BLOCK, head_count * hea...  122 us
    all_gather x1, waiting for transfers between devices, body(): lax.all_gather(queries, 'ka', axis=0, tiled=True)  61.2 us
    psum x1, blocking collectives, body(): row_sum = lax.psum(sweep_pairs(0, pair_total, visit_sum, empty_sum), 'ka')  55.7 us
    all_gather x1, waiting for transfers between devices, body(): lax.all_gather(key_vectors, 'pb', axis=0, tiled=True)  53.8 us
    pmax x1, blocking collectives, body(): row_max = lax.pmax(sweep_pairs(0, pair_total, visit_max, empty_max), 'ka')  48.7 us
  transfers between devices with their start and end apart: 8, of which 6 were waited for; matrix products, arithmetic and copies ran while one was open for 6% of the time, Pallas kernels for 0%

commit v1 on v0

v1 whole, which is shorter than its diff:
```python
import math

import jax
import jax.numpy as jnp
from jax import lax
from jax.experimental import pallas as pl
from jax.experimental.pallas import tpu as pltpu
from jax.sharding import PartitionSpec as P

NX, NY, NZ = 4, 4, 8
PLANE = NY * NZ
SHARDS = 256
NBLK = 512
BLOCK = 64
HD = 128
HEADS = 8
SLOTS = 8
SCALE = 1.0 / math.sqrt(HD)
NEG = -1e30
MESH = pl.DeviceIdType.MESH
F32, BF16 = jnp.float32, jnp.bfloat16


def here():
    pb, ka = lax.axis_index("pb"), lax.axis_index("ka")
    return ka % 4, pb // 8, (ka // 4) * 4 + (pb // 2) % 4, pb % 2


def device(x, y, z, c):
    return ((y * 4 + z % 4) * 2 + c, (z // 4) * 4 + x)


def place(block):
    shard = block // 2
    pb, ka = shard // 8, shard % 8
    return ka % 4, pb % 2, (pb // 8) * 8 + (ka // 4) * 4 + (pb // 2) % 4, block % 2


def remote(src, dst, ssem, rsem, dev):
    return pltpu.make_async_remote_copy(
        src_ref=src, dst_ref=dst, send_sem=ssem, recv_sem=rsem, device_id=dev, device_id_type=MESH
    )


def ring_steps(n):
    last = n // 2 - 1
    return [(d, k, k == last) for k in range(last + 1) for d in (0, 1)]


def gather_flow(piece, half, order, pos, core, sems, arrived):
    x, y, z = pos
    ssem, rsem = sems
    size = {"y": NY, "z": NZ}
    n1, n2 = size[order[0]], size[order[1]]

    def at(o1, o2):
        oy, oz = (o1, o2) if order[0] == "y" else (o2, o1)
        return (y + oy + NY) % NY, (z + oz + NZ) % NZ

    def dev(axis, step):
        if axis == "y":
            return device(x, (y + step + NY) % NY, z, core)
        return device(x, y, (z + step + NZ) % NZ, core)

    def ref(o1, o2, d, halved):
        cy, cz = at(o1, o2)
        return half(cy, cz, d) if halved else piece(cy, cz)

    def copy(o1, o2, d, halved, axis, sem):
        r = ref(o1, o2, d, halved)
        return remote(r, r, ssem.at[sem], rsem.at[sem], dev(axis, 1 if d == 0 else -1))

    offsets = [0]
    for k in range(1, n1 // 2):
        offsets += [-k, k]
    offsets.append(n1 // 2)
    ready = {o: abs(o) for o in offsets}
    plan = {}

    def add(r, what):
        plan.setdefault(r, []).append(what)

    for d, k, halved in ring_steps(n1):
        sign = -1 if d == 0 else 1
        add(k, ("send", sign * k, 0, d, halved, order[0], d * (n1 // 2) + k))
        add(k + 1, ("wait", sign * (k + 1), 0, d, halved, order[0], d * (n1 // 2) + k))
    for i, o in enumerate(offsets):
        for d, k, halved in ring_steps(n2):
            sign = -1 if d == 0 else 1
            sem = n1 + i * n2 + d * (n2 // 2) + k
            add(ready[o] + k, ("send", o, sign * k, d, halved, order[1], sem))
            add(ready[o] + k + 1, ("wait", o, sign * (k + 1), d, halved, order[1], sem))
    sends = []
    for r in range(max(plan) + 1):
        full = set()
        for what, o1, o2, d, halved, axis, sem in plan[r]:
            if what == "wait":
                copy(o1, o2, d, halved, axis, sem).wait_recv()
                if not halved or d == 1:
                    full.add((o1, o2))
        for o1, o2 in sorted(full):
            arrived(*at(o1, o2))
        for what, o1, o2, d, halved, axis, sem in plan[r]:
            if what == "send":
                cp = copy(o1, o2, d, halved, axis, sem)
                cp.start()
                sends.append(cp)
        yield
    for cp in sends:
        cp.wait_send()


GATHER_SEMS = {("y", "z"): NY + NY * NZ, ("z", "y"): NZ + NZ * NY}


def reduce_flow(own, got, out, order, pos, core, sems, done):
    x, y, z = pos
    ssem, rsem = sems
    size = {"y": NY, "z": NZ}
    n1, n2 = size[order[0]], size[order[1]]
    rows = HD // 2

    def at(o1, o2):
        oy, oz = (o1, o2) if order[0] == "y" else (o2, o1)
        return (y + oy + NY) % NY, (z + oz + NZ) % NZ

    def dev(axis, step):
        if axis == "y":
            return device(x, (y + step + NY) % NY, z, core)
        return device(x, y, (z + step + NZ) % NZ, core)

    def copy(src, i, halved, d, axis):
        dst = got.at[i]
        if halved:
            dst = dst.at[pl.ds(d * rows, rows)]
        return remote(src, dst, ssem.at[i], rsem.at[i], dev(axis, 1 if d == 0 else -1))

    def half_of(ref, d):
        return ref.at[pl.ds(d * rows, rows)]

    offsets = [n2 // 2]
    for k in range(n2 // 2 - 1, 0, -1):
        offsets += [-k, k]
    offsets.append(0)
    start = {o: n2 // 2 - abs(o) for o in offsets}
    plan = {}

    def add(r, kind, fn):
        plan.setdefault(r, {}).setdefault(kind, []).append(fn)

    sends = []

    def ring(n, axis, base, r0, term, result):
        steps = n // 2
        for d in (0, 1):
            sign = 1 if d == 0 else -1
            for t in range(steps):
                i = base + d * steps + t
                o = sign * (steps - t)

                def send(i=i, o=o, t=t, d=d):
                    ref, value = term(o)
                    if t == 0:
                        if ref is None:
                            half_of(out.at[i], d)[...] = value(d).astype(BF16)
                            src = half_of(out.at[i], d)
                        else:
                            src = half_of(ref, d)
                        cp = copy(src, i, True, d, axis)
                    else:
                        if t == 1:
                            got_half = half_of(got.at[i - 1], d)[...].astype(F32)
                            half_of(out.at[i], d)[...] = (value(d) + got_half).astype(BF16)
                            half_of(out.at[i], 1 - d)[...] = value(1 - d).astype(BF16)
                        else:
                            out[i] = (value(None) + got[i - 1].astype(F32)).astype(BF16)
                        cp = copy(out.at[i], i, False, d, axis)
                    cp.start()
                    sends.append(cp)

                def wait(i=i, t=t, d=d):
                    src = half_of(out.at[i], d) if t == 0 else out.at[i]
                    copy(src, i, t == 0, d, axis).wait_recv()

                add(r0 + t, "send", send)
                add(r0 + t + 1, "wait", wait)
        result(r0 + steps, base)

    s1, s2 = n1 // 2, n2 // 2
    for j, o2 in enumerate(offsets):

        def term(o1, o2=o2):
            r = own(*at(o1, o2))

            def value(h, r=r):
                return (r[...] if h is None else half_of(r, h)[...]).astype(F32)

            return r, value

        ring(n1, order[0], j * n1, start[o2], term, lambda r, base: None)

    def term2(o2):
        base = offsets.index(abs(o2) if abs(o2) == n2 // 2 else o2) * n1
        a, b = base + s1 - 1, base + n1 - 1

        def value(h):
            r = own(*at(0, o2))
            if h is None:
                return r[...].astype(F32) + got[a].astype(F32) + got[b].astype(F32)
            return (
                half_of(r, h)[...].astype(F32)
                + half_of(got.at[a], h)[...].astype(F32)
                + half_of(got.at[b], h)[...].astype(F32)
            )

        return None, value

    base2 = n1 * n2
    ring(n2, order[1], base2, start[n2 // 2] + s1, term2, lambda r, base: None)
    for r in range(max(plan) + 1):
        for fn in plan[r].get("wait", []):
            fn()
        for fn in plan[r].get("send", []):
            fn()
        yield
    value = term2(0)[1](None)
    value += got[base2 + s2 - 1].astype(F32) + got[base2 + n2 - 1].astype(F32)
    done(value)
    for cp in sends:
        cp.wait_send()


REDUCE_MSGS = {("y", "z"): NY * NZ + NZ, ("z", "y"): NZ * NY + NY}


def run_rounds(*flows):
    flows = list(flows)
    while flows:
        alive = []
        for f in flows:
            try:
                next(f)
                alive.append(f)
            except StopIteration:
                pass
        flows = alive


def greet(devices):
    barrier = pltpu.get_barrier_semaphore()
    for dev in devices:
        pl.semaphore_signal(barrier, inc=1, device_id=dev, device_id_type=MESH)
    pl.semaphore_wait(barrier, len(devices))


def nt(a, b):
    return lax.dot_general(a, b, (((1,), (1,)), ((), ())), preferred_element_type=F32)


def tn(a, b):
    return lax.dot_general(a, b, (((0,), (0,)), ((), ())), preferred_element_type=F32)


def nn(a, b):
    return lax.dot_general(a, b, (((1,), (0,)), ((), ())), preferred_element_type=F32)


def kernel_a(
    rand, glob, rand_any, q, k, v, d,
    att, dq, contrib, gp, gs, gq, gd, near_sum, gout, rand_sib,
    col, gch, sel, xbuf, xsend, near, near_send, near_got, cbuf, stat, part,
    sg, dpg, kc, vc, qs, ds_, dkv, own_sum,
    a_ssem, a_rsem, b_ssem, b_rsem, c_ssem, c_rsem, ssem, rsem, lsem,
):
    x, y, z, c = here()
    pb, ka = lax.axis_index("pb"), lax.axis_index("ka")
    shard = pb * 8 + ka
    me = y * NZ + z
    row = c * 4 + x
    zh = z // 4

    def plane_dev(p):
        return device(x, p // NZ, p % NZ, c)

    def row_dev(r):
        return device(r % 4, y, z, r // 4)

    def shard_dev(s):
        return (s // 8, s % 8)

    nxt, prv = (shard + 1) % SHARDS, (shard + SHARDS - 1) % SHARDS
    row_peers = [(row + i) % 8 for i in range(1, 8)]
    x_peers = [c * 4 + (x + i) % 4 for i in range(1, 4)]
    sibling = row_dev((row + 4) % 8)

    local = [
        pltpu.make_async_copy(k, col.at[c, me, 0], lsem.at[0]),
        pltpu.make_async_copy(v, col.at[c, me, 1], lsem.at[1]),
    ]

    def tile(ref, p):
        return ref.at[:, p % 4, :, pl.ds(pl.multiple_of((p // 4) * HD, HD), HD)]

    local += [
        pltpu.make_async_copy(tile(q, me), gch.at[me, 0], lsem.at[2]),
        pltpu.make_async_copy(tile(d, me), gch.at[me, 1], lsem.at[3]),
    ]
    for cp in local:
        cp.start()
    barrier = pltpu.get_barrier_semaphore()

    def hello(i, carry):
        pl.semaphore_signal(barrier, inc=1, device_id=plane_dev((me + i) % PLANE), device_id_type=MESH)
        return carry

    lax.fori_loop(1, PLANE, hello, 0)
    others = [row_dev(r) for r in row_peers] + [shard_dev(nxt), shard_dev(prv)]
    for dev in others:
        pl.semaphore_signal(barrier, inc=1, device_id=dev, device_id_type=MESH)
    pl.semaphore_wait(barrier, PLANE - 1 + len(others))
    for cp in local:
        cp.wait()

    to_next = remote(
        col.at[c, me, :, 1], near.at[0], ssem.at[0], rsem.at[0], shard_dev(nxt)
    )
    to_prev = remote(
        col.at[c, me, :, 0], near.at[1], ssem.at[1], rsem.at[1], shard_dev(prv)
    )
    rand_copy = remote(rand_any, rand_sib, ssem.at[2], rsem.at[2], sibling)

    def pass_on(kv):
        def arrived(py, pz):
            ref = col.at[c, py * NZ + pz, kv]
            remote(ref, ref, ssem.at[3 + kv], rsem.at[3 + kv], sibling).start()

        return arrived

    def piece(kv):
        return lambda py, pz: col.at[c, py * NZ + pz, kv]

    def half(kv):
        return lambda py, pz, h: col.at[c, py * NZ + pz, kv, h]

    flow_k = gather_flow(piece(0), half(0), ("y", "z"), (x, y, z), c, (a_ssem, a_rsem), pass_on(0))
    flow_v = gather_flow(piece(1), half(1), ("z", "y"), (x, y, z), c, (b_ssem, b_rsem), pass_on(1))
    next(flow_k)
    next(flow_v)
    pass_on(0)(y, z)
    pass_on(1)(y, z)

    def send_tiles(i, carry):
        p = (me + i) % PLANE
        remote(tile(q, p), gch.at[me, 0], ssem.at[5], rsem.at[5], plane_dev(p)).start()
        remote(tile(d, p), gch.at[me, 1], ssem.at[5], rsem.at[5], plane_dev(p)).start()
        return carry

    lax.fori_loop(1, PLANE, send_tiles, 0)
    to_next.start()
    to_prev.start()
    rand_copy.start()

    for j in range(2):
        for h in range(HEADS):
            rows = pl.ds(j * 512 + h * 64, 64)
            qs[rows, :] = q[j, :, :, h * HD : (h + 1) * HD].reshape(64, HD)
            ds_[rows, :] = d[j, :, :, h * HD : (h + 1) * HD].reshape(64, HD)

    run_rounds(flow_k, flow_v)
    tiles_in = remote(gch.at[pl.ds(0, 31)], gch.at[pl.ds(0, 31)], ssem.at[5], rsem.at[5], sibling)
    tiles_in.wait_recv()

    g_place = [place(glob[g]) for g in range(2)]
    for g in range(2):
        gx, gc, gpl, gh = g_place[g]
        for t in range(2):
            sel[row, g, t] = gch[gpl, t, gh]
    for r in row_peers:
        remote(sel.at[row], sel.at[row], ssem.at[6], rsem.at[6], row_dev(r)).start()

    for kv in range(2):
        remote(col.at[1 - c, :, kv], col.at[1 - c, :, kv], ssem.at[3 + kv], rsem.at[3 + kv], sibling).wait_recv()

    def wanted(ka_of, slot):
        if slot >= 6:
            return glob[slot - 6]
        return rand[ka_of * 2 + slot // 3, slot % 3]

    for i in range(1, 4):
        xd = (x + i) % 4
        for slot in range(SLOTS):
            bx, bc, bp, bh = place(wanted(zh * 4 + xd, slot))
            for kv in range(2):
                xsend[i - 1, slot, kv] = col[bc, bp, kv, bh]
        remote(xsend.at[i - 1], xbuf.at[x], ssem.at[7], rsem.at[7], row_dev(c * 4 + xd)).start()
    for slot in range(SLOTS):
        bx, bc, bp, bh = place(wanted(ka, slot))
        for kv in range(2):
            xbuf[x, slot, kv] = col[bc, bp, kv, bh]

    remote(sel.at[pl.ds(0, 7)], sel.at[pl.ds(0, 7)], ssem.at[6], rsem.at[6], sibling).wait_recv()
    for g in range(2):
        gx, gc, gpl, gh = g_place[g]
        gq[pl.ds(g * 16, 16), :] = sel[gc * 4 + gx, g, 0]
        gd[pl.ds(g * 16, 16), :] = sel[gc * 4 + gx, g, 1]

    def g_scores(p, carry):
        lanes = pl.ds(pl.multiple_of(p * HD, HD), HD)
        sg[:, lanes] = nt(gq[...], col[c, p, 0].reshape(HD, HD)) * SCALE
        dpg[:, lanes] = nt(gd[...], col[c, p, 1].reshape(HD, HD))
        return carry

    lax.fori_loop(0, PLANE, g_scores, 0)
    g_max = jnp.max(sg[...], axis=1, keepdims=True)
    g_exp = jnp.exp(sg[...] - g_max)
    g_sum = jnp.sum(g_exp, axis=1, keepdims=True)
    g_dot = jnp.sum(g_exp * dpg[...], axis=1, keepdims=True)
    lane = lax.broadcasted_iota(jnp.int32, (32, HD), 1)
    stat[row] = jnp.where(lane == 0, g_max, jnp.where(lane == 1, g_sum, g_dot))
    for r in row_peers:
        remote(stat.at[row], stat.at[row], ssem.at[8], rsem.at[8], row_dev(r)).start()

    to_next.wait_recv()
    to_prev.wait_recv()
    remote(xbuf.at[pl.ds(0, 3)], xbuf.at[pl.ds(0, 3)], ssem.at[7], rsem.at[7], sibling).wait_recv()
    slot_of = lax.broadcasted_iota(jnp.int32, (1, 512), 1) // BLOCK
    lo, hi = pl.ds(0, BLOCK), pl.ds(BLOCK, BLOCK)
    for j in range(2):
        block = shard * 2 + j
        cand = [block - 1, block, block + 1, glob[0], glob[1]]
        cand += [rand[ka * 2 + j, r] for r in range(3)]
        for kv, dst in ((0, kc), (1, vc)):
            near_refs = [near.at[0, kv], col.at[c, me, kv, 0], col.at[c, me, kv, 1], near.at[1, kv]]
            for i in range(3):
                dst[i * BLOCK : (i + 1) * BLOCK, :] = near_refs[i + j][...]
            for i in range(3, 8):
                slot = 6 + i - 3 if i < 5 else j * 3 + i - 5
                dst[i * BLOCK : (i + 1) * BLOCK, :] = xbuf[place(cand[i])[0], slot, kv]
        cands = jnp.zeros((1, 512), jnp.int32)
        for i in range(8):
            cands = jnp.where(slot_of == i, cand[i], cands)
        out = (cands < 0) | (cands >= NBLK)
        for i in range(7):
            out = out | ((slot_of > i) & (cands == cand[i]))
        bias = jnp.where(out, NEG, 0.0)
        blocks = jnp.full((256, 1), block, jnp.int32)
        keep = jnp.where((blocks == glob[0]) | (blocks == glob[1]), 0.0, 1.0)
        for part_i in range(2):
            rows = pl.ds(j * 512 + part_i * 256, 256)
            qv, dv = qs[rows, :], ds_[rows, :]
            s = nt(qv, kc[...]) * SCALE + bias
            e = jnp.exp(s - jnp.max(s, axis=1, keepdims=True))
            w = e * (keep / jnp.sum(e, axis=1, keepdims=True))
            wb = w.astype(BF16)
            o = nn(wb, vc[...]).astype(BF16)
            dot = jnp.sum(dv.astype(F32) * o.astype(F32), axis=1, keepdims=True)
            ds = (w * (nt(dv, vc[...]) - dot)).astype(BF16)
            dqv = (nn(ds, kc[...]) * SCALE).astype(BF16)
            for h in range(4):
                cols = slice((part_i * 4 + h) * HD, (part_i * 4 + h + 1) * HD)
                att[j, :, :, cols] = o[h * 64 : (h + 1) * 64].reshape(4, 16, HD)
                dq[j, :, :, cols] = dqv[h * 64 : (h + 1) * 64].reshape(4, 16, HD)
            dk_new, dv_new = tn(ds, qv) * SCALE, tn(wb, dv)
            if part_i == 0:
                dkv[0], dkv[1] = dk_new, dv_new
            else:
                dkv[0] += dk_new
                dkv[1] += dv_new
        for kv in range(2):
            for i in range(8):
                term = dkv[kv, i * BLOCK : (i + 1) * BLOCK, :]
                spot = i + j - 1
                if i < 3 and spot in (-1, 2):
                    near_send[0 if spot == -1 else 1, kv] = term.astype(BF16)
                elif i < 3:
                    if (j, i) in ((0, 1), (0, 2)):
                        own_sum[kv, pl.ds(spot * BLOCK, BLOCK), :] = term
                    else:
                        own_sum[kv, pl.ds(spot * BLOCK, BLOCK), :] += term
                elif i >= 5:
                    cbuf[row, j * 3 + i - 5, kv] = term.astype(BF16)
                elif j == 0:
                    own_sum[2 + kv, pl.ds((i - 3) * BLOCK, BLOCK), :] = term
                else:
                    total = own_sum[2 + kv, pl.ds((i - 3) * BLOCK, BLOCK), :] + term
                    cbuf[row, 6 + i - 3, kv] = total.astype(BF16)

    def c_copy(src, h, step, sem):
        ref = cbuf.at[src] if h is None else cbuf.at[src, pl.ds(h * 4, 4)]
        dev = sibling if step is None else row_dev(c * 4 + (x + step + 4) % 4)
        return remote(ref, ref, c_ssem.at[sem], c_rsem.at[sem], dev)

    at_x = lambda o: c * 4 + (x + o + 4) % 4
    to_back = remote(near_send.at[0], near_got.at[1], ssem.at[9], rsem.at[9], shard_dev(prv))
    to_fore = remote(near_send.at[1], near_got.at[0], ssem.at[10], rsem.at[10], shard_dev(nxt))
    c_sends = [c_copy(row, None, 1, 0), c_copy(row, None, -1, 1), c_copy(row, None, None, 4)]
    for cp in c_sends:
        cp.start()
    to_back.start()
    to_fore.start()

    remote(stat.at[pl.ds(0, 7)], stat.at[pl.ds(0, 7)], ssem.at[8], rsem.at[8], sibling).wait_recv()
    stats = [stat[i] for i in range(8)]
    top = stats[0][:, 0:1]
    for i in range(1, 8):
        top = jnp.maximum(top, stats[i][:, 0:1])
    total, dot = jnp.zeros((32, 1), F32), jnp.zeros((32, 1), F32)
    for i in range(8):
        f = jnp.exp(stats[i][:, 0:1] - top)
        total += stats[i][:, 1:2] * f
        dot += stats[i][:, 2:3] * f
    g_row = lax.broadcasted_iota(jnp.int32, (32, 1), 0)
    g_one = jnp.full((32, 1), glob[1], jnp.int32)
    first = jnp.where((g_row >= 16) & (g_one == glob[0]), 0.0, 1.0)
    gw = jnp.exp(sg[...] - top) * (first / total)
    gp[...] = gw.astype(BF16)
    gs[...] = (gw * (dpg[...] - dot / total)).astype(BF16)

    def g_out(p, carry):
        lanes = pl.ds(pl.multiple_of(p * HD, HD), HD)
        o, dqv = carry
        return o + nn(gp[:, lanes], col[c, p, 1].reshape(HD, HD)), dqv + nn(gs[:, lanes], col[c, p, 0].reshape(HD, HD))

    zero = jnp.zeros((32, HD), F32)
    g_o, g_dq = lax.fori_loop(0, PLANE, g_out, (zero, zero))
    part[row, 0] = g_o
    part[row, 1] = g_dq * SCALE
    for r in row_peers:
        remote(part.at[row], part.at[row], ssem.at[11], rsem.at[11], row_dev(r)).start()

    c_copy(at_x(-1), None, 1, 0).wait_recv()
    c_copy(at_x(1), None, -1, 1).wait_recv()
    more = [
        c_copy(at_x(-1), 0, 1, 2), c_copy(at_x(1), 1, -1, 3),
        c_copy(at_x(-1), None, None, 5), c_copy(at_x(1), None, None, 6),
    ]
    for cp in more:
        cp.start()
    c_sends += more
    c_copy(at_x(2), 0, 1, 2).wait_recv()
    c_copy(at_x(2), 1, -1, 3).wait_recv()
    last = c_copy(at_x(2), None, None, 7)
    last.start()
    c_sends.append(last)

    remote(part.at[pl.ds(0, 7)], part.at[pl.ds(0, 7)], ssem.at[11], rsem.at[11], sibling).wait_recv()
    for t in range(2):
        acc = part[0, t]
        for i in range(1, 8):
            acc += part[i, t]
        for g in range(2):
            gout[t, g] = acc[g * 16 : (g + 1) * 16].astype(BF16)
    to_back.wait_recv()
    to_fore.wait_recv()
    for kv in range(2):
        near_sum[kv, lo, :] = own_sum[kv, lo, :] + near_got[0, kv].astype(F32)
        near_sum[kv, hi, :] = own_sum[kv, hi, :] + near_got[1, kv].astype(F32)

    def at_other(o):
        return (1 - c) * 4 + (x + o + 4) % 4

    for sem, o in ((4, 0), (5, -1), (6, 1), (7, 2)):
        c_copy(at_other(o), None, None, sem).wait_recv()
    out_copy = pltpu.make_async_copy(cbuf, contrib, lsem.at[0])
    out_copy.start()
    out_copy.wait()
    rand_copy.wait_recv()

    for cp in c_sends + [to_next, to_prev, rand_copy, to_back, to_fore]:
        cp.wait_send()
    for kv in range(2):
        remote(col.at[c, :, kv], col.at[c, :, kv], ssem.at[3 + kv], rsem.at[3 + kv], sibling).wait_send()
    tiles_in.wait_send()
    for ref, sem, n in ((sel, 6, 7), (xbuf, 7, 3), (stat, 8, 7), (part, 11, 7)):
        remote(ref.at[pl.ds(0, n)], ref.at[pl.ds(0, n)], ssem.at[sem], rsem.at[sem], sibling).wait_send()


def kernel_b(rand, rand_sib, glob, contrib, gp, gs, gq, gd, out, acc):
    x, y, z, c = here()
    zh = z // 4

    def dense(p, carry):
        lanes = pl.ds(pl.multiple_of(p * HD, HD), HD)
        acc[p, 0] = tn(gs[:, lanes], gq[...]) * SCALE
        acc[p, 1] = tn(gp[:, lanes], gd[...])
        return carry

    lax.fori_loop(0, PLANE, dense, 0)
    for core in range(2):
        for xs in range(NX):
            for slot in range(SLOTS):
                if slot >= 6:
                    block = glob[slot - 6]
                else:
                    r, s = (zh * 4 + xs) * 2 + slot // 3, slot % 3
                    block = jnp.where(c == core, rand[r, s], rand_sib[r, s])
                bx, bc, bp, bh = place(block)

                @pl.when((bx == x) & (bc == c))
                def _(core=core, xs=xs, slot=slot, bp=bp, bh=bh):
                    rows = pl.ds(pl.multiple_of(bh * BLOCK, BLOCK), BLOCK)
                    src = jnp.where(core == 0, 0, 4) + xs
                    acc[bp, :, rows, :] += contrib[src, slot].astype(F32)

    def narrow(p, carry):
        out[p] = acc[p].astype(BF16)
        return carry

    lax.fori_loop(0, PLANE, narrow, 0)


def kernel_c(
    glob, acc, near_sum, att_in, dq_in, gout,
    att, dq, dk, dv,
    got_k, out_k, got_v, out_v, gall,
    k_ssem, k_rsem, v_ssem, v_rsem, o_ssem, o_rsem, w_ssem, w_rsem, lsem,
):
    x, y, z, c = here()
    me = y * NZ + z
    shard = lax.axis_index("pb") * 8 + lax.axis_index("ka")
    own = pltpu.make_async_copy(gout, gall.at[me], lsem.at[0])
    own.start()
    greet(
        [
            device(x, (y + 1) % NY, z, c), device(x, (y + NY - 1) % NY, z, c),
            device(x, y, (z + 1) % NZ, c), device(x, y, (z + NZ - 1) % NZ, c),
        ]
    )
    own.wait()
    pos = (x, y, z)

    def finish(kv, dst):
        def done(value):
            dst[...] = (value + near_sum[kv]).astype(BF16)

        return done

    def term(kv):
        return lambda py, pz: acc.at[py * NZ + pz, kv]

    def piece(t):
        return lambda py, pz: gall.at[py * NZ + pz, t]

    def half(t):
        return lambda py, pz, h: gall.at[py * NZ + pz, t, h]

    nothing = lambda py, pz: None
    run_rounds(
        reduce_flow(term(0), got_k, out_k, ("z", "y"), pos, c, (k_ssem, k_rsem), finish(0, dk)),
        reduce_flow(term(1), got_v, out_v, ("y", "z"), pos, c, (v_ssem, v_rsem), finish(1, dv)),
        gather_flow(piece(0), half(0), ("y", "z"), pos, c, (o_ssem, o_rsem), nothing),
        gather_flow(piece(1), half(1), ("z", "y"), pos, c, (w_ssem, w_rsem), nothing),
    )
    for j in range(2):
        blocks = jnp.full((16, HD), shard * 2 + j, jnp.int32)
        is_glob = [blocks == glob[g] for g in range(2)]
        for t, src, dst in ((0, att_in, att), (1, dq_in, dq)):
            for p in range(PLANE):
                cols = slice((p // 4) * HD, (p // 4 + 1) * HD)
                value = jnp.where(is_glob[1], gall[p, t, 1], src[j, p % 4, :, cols])
                dst[j, p % 4, :, cols] = jnp.where(is_glob[0], gall[p, t, 0], value)


def body(queries, key_vectors, value_vectors, out_grad, rand_blocks, global_blocks):
    vmem = pl.BlockSpec(memory_space=pltpu.VMEM)
    smem = pl.BlockSpec(memory_space=pltpu.SMEM)
    hbm = pl.BlockSpec(memory_space=pl.ANY)
    shape = jax.ShapeDtypeStruct
    dma = pltpu.SemaphoreType.DMA
    q4 = queries.reshape(2, 4, 16, HEADS * HD)
    d4 = out_grad.reshape(2, 4, 16, HEADS * HD)
    yz, zy = ("y", "z"), ("z", "y")
    ga, gb = GATHER_SEMS[yz], GATHER_SEMS[zy]
    att, dq, contrib, gp, gs, gq, gd, near_sum, gout, rand_sib = pl.pallas_call(
        kernel_a,
        name="exchange_and_attend",
        out_shape=(
            shape((2, 4, 16, HEADS * HD), BF16),
            shape((2, 4, 16, HEADS * HD), BF16),
            shape((8, SLOTS, 2, BLOCK, HD), BF16),
            shape((32, PLANE * HD), BF16),
            shape((32, PLANE * HD), BF16),
            shape((32, HD), BF16),
            shape((32, HD), BF16),
            shape((2, HD, HD), F32),
            shape((2, 2, 16, HD), BF16),
            shape((16, 3), jnp.int32),
        ),
        in_specs=[smem, smem, hbm, vmem, vmem, vmem, vmem],
        out_specs=(vmem, vmem, hbm, vmem, vmem, vmem, vmem, vmem, vmem, hbm),
        scratch_shapes=[
            pltpu.VMEM((2, PLANE, 2, 2, BLOCK, HD), BF16),
            pltpu.VMEM((PLANE, 2, 2, 16, HD), BF16),
            pltpu.VMEM((8, 2, 2, 16, HD), BF16),
            pltpu.VMEM((4, SLOTS, 2, BLOCK, HD), BF16),
            pltpu.VMEM((3, SLOTS, 2, BLOCK, HD), BF16),
            pltpu.VMEM((2, 2, BLOCK, HD), BF16),
            pltpu.VMEM((2, 2, BLOCK, HD), BF16),
            pltpu.VMEM((2, 2, BLOCK, HD), BF16),
            pltpu.VMEM((8, SLOTS, 2, BLOCK, HD), BF16),
            pltpu.VMEM((8, 32, HD), F32),
            pltpu.VMEM((8, 2, 32, HD), F32),
            pltpu.VMEM((32, PLANE * HD), F32),
            pltpu.VMEM((32, PLANE * HD), F32),
            pltpu.VMEM((512, HD), BF16),
            pltpu.VMEM((512, HD), BF16),
            pltpu.VMEM((1024, HD), BF16),
            pltpu.VMEM((1024, HD), BF16),
            pltpu.VMEM((2, 512, HD), F32),
            pltpu.VMEM((4, HD, HD), F32),
            dma((ga,)), dma((ga,)), dma((gb,)), dma((gb,)), dma((8,)), dma((8,)),
            dma((12,)), dma((12,)), dma((4,)),
        ],
        compiler_params=pltpu.CompilerParams(collective_id=0, has_side_effects=True),
    )(
        rand_blocks, global_blocks, rand_blocks, q4,
        key_vectors.reshape(2, BLOCK, HD), value_vectors.reshape(2, BLOCK, HD), d4,
    )
    acc = pl.pallas_call(
        kernel_b,
        name="spread_terms",
        out_shape=shape((PLANE, 2, HD, HD), BF16),
        in_specs=[smem, smem, smem, vmem, vmem, vmem, vmem, vmem],
        out_specs=vmem,
        scratch_shapes=[pltpu.VMEM((PLANE, 2, HD, HD), F32)],
    )(rand_blocks, rand_sib, global_blocks, contrib, gp, gs, gq, gd)
    mk, mv = REDUCE_MSGS[zy], REDUCE_MSGS[yz]
    att, dq, dk, dv = pl.pallas_call(
        kernel_c,
        name="reduce_and_finish",
        out_shape=(
            shape((2, 4, 16, HEADS * HD), BF16),
            shape((2, 4, 16, HEADS * HD), BF16),
            shape((HD, HD), BF16),
            shape((HD, HD), BF16),
        ),
        in_specs=[smem] + [vmem] * 5,
        out_specs=(vmem,) * 4,
        scratch_shapes=[
            pltpu.VMEM((mk, HD, HD), BF16), pltpu.VMEM((mk, HD, HD), BF16),
            pltpu.VMEM((mv, HD, HD), BF16), pltpu.VMEM((mv, HD, HD), BF16),
            pltpu.VMEM((PLANE, 2, 2, 16, HD), BF16),
            dma((mk,)), dma((mk,)), dma((mv,)), dma((mv,)),
            dma((ga,)), dma((ga,)), dma((gb,)), dma((gb,)), dma((1,)),
        ],
        compiler_params=pltpu.CompilerParams(collective_id=1, has_side_effects=True),
    )(global_blocks, acc, near_sum, att, dq, gout)
    return att.reshape(queries.shape), dq.reshape(queries.shape), dk, dv


def solution(mesh):
    assert (mesh.shape["pb"], mesh.shape["ka"]) == (32, 8)
    rows = P(("pb", "ka"), None)
    return jax.shard_map(
        body,
        mesh=mesh,
        in_specs=(rows, rows, rows, rows, P("pb", None), P()),
        out_specs=(rows, rows, rows, rows),
        check_vma=False,
    )
```

time: 1300 us -> 142 us (0.11)
  waiting for transfers between devices: 1010 us -> 0 us
  blocking collectives: 145 us -> 0 us
  Pallas kernels: 0 us -> 132 us
  local copies, waits for them, and re-layouts: 68.5 us -> 7.44 us
  other arithmetic: 37.5 us -> 0 us
  matrix products: 18.8 us -> 0 us
  between operations: 15 us -> 0.65 us
    reduce_scatter x4 -> x0, waiting for transfers between devices: 892 us -> none  [the longest x1 327 us: body(): lax.psum_scatter(value_acc.reshape(key_blocks * BLOCK, head_dim), 'pb', s...]
    pallas_call x0 -> x3, Pallas kernels: none -> 132 us  [the longest x1 85.1 us: body(): pl.pallas_call(kernel_a, name='exchange_and_attend', out_shape=(shape((2,...]
    all_gather x4 -> x0, waiting for transfers between devices: 115 us -> none  [the longest x1 61.2 us: body(): lax.all_gather(queries, 'ka', axis=0, tiled=True)]
    psum x1 -> x0, blocking collectives: 55.7 us -> none  [body(): row_sum = lax.psum(sweep_pairs(0, pair_total, visit_sum, empty_sum), 'ka')]
    pmax x1 -> x0, blocking collectives: 48.7 us -> none  [body(): row_max = lax.pmax(sweep_pairs(0, pair_total, visit_max, empty_max), 'ka')]
    all_gather x1 -> x0, blocking collectives: 40.2 us -> none  [body(): lax.all_gather(own_dots, 'ka', axis=0, tiled=True)]
    gather x17 -> x0, local copies, waits for them, and re-layouts: 27.5 us -> none  [the longest x4 8.71 us: scores(): q_sel = q_grid[row_ids]]
    scatter-add x5 -> x0, other arithmetic: 24.8 us -> none  [the longest x1 9.07 us: visit_out(): return totals.at[target].add(partial_value)]
  transfers between devices with their start and end apart: 8 -> 0, of which waited for: 6 -> 0; matrix products, arithmetic and copies ran while one was open for 6% -> 0% of each run, Pallas kernels for 0% -> 0%
where the time goes in v1:
time: 142 us; the launch traced here: 140 us
  Pallas kernels  132 us (93%)
  local copies, waits for them, and re-layouts  7.44 us (5%)
    pallas_call x1, Pallas kernels, body(): pl.pallas_call(kernel_a, name='exchange_and_attend', out_shape=(shape((2,...  85.1 us
    pallas_call x1, Pallas kernels, body(): pl.pallas_call(kernel_c, name='reduce_and_finish', out_shape=(shape((2, 4...  34.6 us
    pallas_call x1, Pallas kernels, body(): pl.pallas_call(kernel_b, name='spread_terms', out_shape=shape((PLANE, 2,...  12.5 us
    unnamed x5, local copies, waits for them, and re-layouts  7.44 us

profile of v1, /device:TPU:2, one launch (start us, length us, event | category | flops | bytes accessed | tf_op | source)
XLA Modules:
  0.0 140.3 jit_solution(8419452007350236190)
XLA Ops:
  0.6 1.4 copy.12.rand.rand_any
  2.0 85.1 %exchange_and_attend.1 = (bf16[2,4,16,1024]{3,2,1,0:T(8,128)(2,1)}, bf16[2,4,16,1024]{3,2,1,0:T(8,128)(2,1)}, bf16[8,8,2,64,128]{4,3,2,1,0:T(8,128)(2,1)}, bf16[...) custom-call(s32[16,3]{1,0:T(8,128)} %copy.12.rand.rand_any, ...), custom_call_target="tpu_custom_call" | custom-call | tf_op jit(solution)/shard_map/exchange_and_attend/pallas_call | solution.py:674
  87.1 12.5 %spread_terms.1.acc = bf16[32,2,128,128]{3,2,1,0:T(8,128)(2,1)} custom-call(s32[16,3]{1,0:T(8,128)} %copy.12.rand.rand_any, s32[16,3]{1,0:T(8,128)} %get-tuple-element.18.rand_sib, s32[2]{0:T(128)} %glob.5, bf16[8,8,2,64,128]{4,3,2,1,0:T(8,128)(2,1)} %get-tuple-element.19.contrib, bf16[32,4096]{1,0:T(8,128)(2,1)} %get-tuple-element.20.gp, ...), custom_call_target="tpu_custom_call" | custom-call | tf_op jit(solution)/shard_map/spread_terms/pallas_call | solution.py:719
  99.5 34.6 %reduce_and_finish.1 = (bf16[2,4,16,1024]{3,2,1,0:T(8,128)(2,1)}, bf16[2,4,16,1024]{3,2,1,0:T(8,128)(2,1)}, bf16[128,128]{1,0:T(8,128)(2,1)}, bf16[128,128]{1,0:T(8,128)(2,1)}) custom-call(s32[2]{0:T(128)} %glob.5, bf16[32,2,128,128]{3,2,1,0:T(8,128)(2,1)} %spread_terms.1.acc, f32[2,128,128]{2,1,0:T(8,128)} %get-tuple-element.24.near_sum, ...), custom_call_target="tpu_custom_call" | custom-call | tf_op jit(solution)/shard_map/reduce_and_finish/pallas_call | solution.py:728
  134.2 1.7 %copy.17 = bf16[128,1024]{1,0:T(8,128)(2,1)} copy(bf16[128,1024]{1,0:T(8,128)(2,1)} %bitcast.9) | data formatting | bytes 524288
  135.9 1.7 %copy.18 = bf16[128,1024]{1,0:T(8,128)(2,1)} copy(bf16[128,1024]{1,0:T(8,128)(2,1)} %bitcast.8) | data formatting | bytes 524288
  137.5 1.4 copy.19
  138.9 1.4 copy.20

commit v2 on v1

v2 whole, which is shorter than its diff:
```python
import math

import jax
import jax.numpy as jnp
from jax import lax
from jax.experimental import pallas as pl
from jax.experimental.pallas import tpu as pltpu
from jax.sharding import PartitionSpec as P

NX, NY, NZ = 4, 4, 8
PLANE = NY * NZ
SHARDS = 256
NBLK = 512
BLOCK = 64
HD = 128
HEADS = 8
SLOTS = 8
SCALE = 1.0 / math.sqrt(HD)
NEG = -1e30
VMEM_A, VMEM_B, VMEM_C, VMEM_D = 28 << 20, 14 << 20, 14 << 20, 8 << 20
MESH = pl.DeviceIdType.MESH
F32, BF16 = jnp.float32, jnp.bfloat16


def here():
    pb, ka = lax.axis_index("pb"), lax.axis_index("ka")
    return ka % 4, pb // 8, (ka // 4) * 4 + (pb // 2) % 4, pb % 2


def device(x, y, z, c):
    return ((y * 4 + z % 4) * 2 + c, (z // 4) * 4 + x)


def place(block):
    shard = block // 2
    pb, ka = shard // 8, shard % 8
    return ka % 4, pb % 2, (pb // 8) * 8 + (ka // 4) * 4 + (pb // 2) % 4, block % 2


def remote(src, dst, ssem, rsem, dev):
    return pltpu.make_async_remote_copy(
        src_ref=src, dst_ref=dst, send_sem=ssem, recv_sem=rsem, device_id=dev, device_id_type=MESH
    )


RATE, LATENCY, AHEAD = 37.0, 1.6, 2.0


def schedule(msgs):
    depth = [1] * len(msgs)
    for i in range(len(msgs) - 1, -1, -1):
        for dep in msgs[i][0]:
            depth[dep] = max(depth[dep], depth[i] + 1)
    ranked = sorted(range(len(msgs)), key=lambda i: (-depth[i], i))
    now, free, arrival, come, order = 0.0, {}, {}, set(), []
    while len(come) < len(msgs):
        for i in ranked:
            deps, link, size, work = msgs[i][:4]
            begin = max(free.get(link, 0.0), now)
            if i in arrival or begin > now + AHEAD or any(dep not in come for dep in deps):
                continue
            now += work
            free[link] = max(begin, now) + size / RATE
            arrival[i] = free[link] + LATENCY
            order.append(("send", i))
        i = min((i for i in arrival if i not in come), key=lambda i: (arrival[i], i))
        now = max(now, arrival[i]) + 0.05
        come.add(i)
        order.append(("wait", i))
    return order


def play(*flows):
    msgs = []
    for own, end in flows:
        base = len(msgs)
        msgs += [([dep + base for dep in m[0]],) + m[1:] for m in own]
    for what, i in schedule(msgs):
        msgs[i][4 if what == "send" else 5]()
    for own, end in flows:
        end()


def ring_around(order, pos, core):
    x, y, z = pos

    def at(o1, o2):
        oy, oz = (o1, o2) if order[0] == "y" else (o2, o1)
        return (y + oy + NY) % NY, (z + oz + NZ) % NZ

    def dev(axis, d):
        step = 1 if d == 0 else -1
        if axis == "y":
            return device(x, (y + step + NY) % NY, z, core)
        return device(x, y, (z + step + NZ) % NZ, core)

    return at, dev, RING[order[0]], RING[order[1]]


RING = {"y": NY, "z": NZ}


def gather_flow(piece, half, order, pos, core, sems, arrived, kb, whole):
    ssem, rsem = sems
    at, dev, n1, n2 = ring_around(order, pos, core)
    msgs, index, seen = [], {}, {}

    def message(deps, o1, o2, nxt, d, halved, axis):
        i = len(msgs)

        def copy(a, b):
            cy, cz = at(a, b)
            ref = half(cy, cz, d) if halved else piece(cy, cz)
            return remote(ref, ref, ssem.at[0], rsem.at[i], dev(axis, d))

        def send():
            copy(o1, o2).start()

        def wait():
            copy(*nxt).wait_recv()
            spot = tuple(abs(o) if abs(o) == n // 2 else o for o, n in zip(nxt, (n1, n2)))
            seen[spot] = seen.get(spot, 0) + 1
            if seen[spot] == (2 if halved else 1):
                arrived(*at(*nxt))

        msgs.append((deps, (axis, d), kb / 2 if halved else kb, 0.02, send, wait))
        return i

    for k in range(n1 // 2):
        for d in (0, 1):
            sign = -1 if d == 0 else 1
            deps = [index[1, sign * k, d]] if k else []
            i = message(deps, sign * k, 0, (sign * (k + 1), 0), d, k == n1 // 2 - 1, order[0])
            index[1, sign * (k + 1), d] = i
    offsets = [0] + [s * k for k in range(1, n1 // 2) for s in (-1, 1)] + [n1 // 2]
    for o in offsets:
        if o == 0:
            first = []
        elif o == n1 // 2:
            first = [index[1, -o, 0], index[1, o, 1]]
        else:
            first = [index[1, o, 0 if o < 0 else 1]]
        for k in range(n2 // 2):
            for d in (0, 1):
                sign = -1 if d == 0 else 1
                deps = [index[2, o, sign * k, d]] if k else first
                i = message(deps, o, sign * k, (o, sign * (k + 1)), d, k == n2 // 2 - 1, order[1])
                index[2, o, sign * (k + 1), d] = i

    def end():
        remote(whole, whole, ssem.at[0], rsem.at[0], dev("y", 0)).wait_send()

    return msgs, end


GATHER_SEMS = {("y", "z"): NY + NY * NZ, ("z", "y"): NZ + NZ * NY}


def reduce_flow(own, got, out, order, pos, core, sems, done, kb):
    ssem, rsem = sems
    at, dev, n1, n2 = ring_around(order, pos, core)
    rows = got.shape[1] // 2
    msgs = []

    def half_of(ref, d):
        return ref.at[pl.ds(d * rows, rows)]

    def load(ref, h):
        return (ref[...] if h is None else half_of(ref, h)[...]).astype(F32)

    def ring(n, axis, term, deps_of):
        steps = n // 2
        base = len(msgs)
        for d in (0, 1):
            for t in range(steps):
                o = (1 if d == 0 else -1) * (steps - t)
                i = base + d * steps + t
                deps = list(deps_of(o)) + ([i - 1] if t else [])

                def copy(i=i, t=t, d=d):
                    src, dst = out.at[i], got.at[i]
                    if t == 0:
                        src, dst = half_of(src, d), half_of(dst, d)
                    return remote(src, dst, ssem.at[0], rsem.at[i], dev(axis, d))

                def send(i=i, o=o, t=t, d=d, copy=copy):
                    value = term(o)
                    if t == 0:
                        half_of(out.at[i], d)[...] = value(d).astype(BF16)
                    elif t == 1:
                        half_of(out.at[i], d)[...] = (value(d) + load(got.at[i - 1], d)).astype(BF16)
                        half_of(out.at[i], 1 - d)[...] = value(1 - d).astype(BF16)
                    else:
                        out[i] = (value(None) + load(got.at[i - 1], None)).astype(BF16)
                    copy().start()

                def wait(copy=copy):
                    copy().wait_recv()

                msgs.append((deps, (axis, d), kb if t else kb / 2, 0.005 * kb, send, wait))
        return base

    offsets = [n2 // 2] + [s * k for k in range(n2 // 2 - 1, 0, -1) for s in (-1, 1)] + [0]
    ends = {}
    for o2 in offsets:

        def term(o1, o2=o2):
            ref = own(*at(o1, o2))
            return lambda h: load(ref, h)

        base = ring(n1, order[0], term, lambda o: [])
        ends[o2] = (base + n1 // 2 - 1, base + n1 - 1)
    ends[-(n2 // 2)] = ends[n2 // 2]

    def term2(o2):
        a, b = ends[o2]
        ref = own(*at(0, o2))
        return lambda h: load(ref, h) + load(got.at[a], h) + load(got.at[b], h)

    base = ring(n2, order[1], term2, lambda o: ends[o])

    def end():
        last = (base + n2 // 2 - 1, base + n2 - 1)
        done(term2(0)(None) + load(got.at[last[0]], None) + load(got.at[last[1]], None))
        whole = out.at[pl.ds(0, PLANE - 1)]
        remote(whole, whole, ssem.at[0], rsem.at[0], dev("y", 0)).wait_send()

    return msgs, end


REDUCE_MSGS = {("y", "z"): NY * NZ + NZ, ("z", "y"): NZ * NY + NY}


def greet(devices):
    barrier = pltpu.get_barrier_semaphore()
    for dev in devices:
        pl.semaphore_signal(barrier, inc=1, device_id=dev, device_id_type=MESH)
    pl.semaphore_wait(barrier, len(devices))


def nt(a, b):
    return lax.dot_general(a, b, (((1,), (1,)), ((), ())), preferred_element_type=F32)


def tn(a, b):
    return lax.dot_general(a, b, (((0,), (0,)), ((), ())), preferred_element_type=F32)


def nn(a, b):
    return lax.dot_general(a, b, (((1,), (0,)), ((), ())), preferred_element_type=F32)


def kernel_a(
    rand_any, glob_any, q_any, k, v, d_any,
    att, dq, contrib, dense, near_sum, gout, rand_sib,
    col, gown, g_got, g_out_buf, sel, xm, xs, xall, stat, part,
    rand, glob, q, d, sg, dpg, gp, gs, gq, gd, kc, vc, qs, ds_, dkv, own_sum,
    a_ssem, a_rsem, b_ssem, b_rsem, g_ssem, g_rsem, c_ssem, c_rsem, x_ssem, x_rsem, ssem, rsem, lsem,
):
    x, y, z, c = here()
    pb, ka = lax.axis_index("pb"), lax.axis_index("ka")
    shard = pb * 8 + ka
    me = y * NZ + z
    row = c * 4 + x
    zh = z // 4
    pos = (x, y, z)

    def row_dev(r):
        return device(r % 4, y, z, r // 4)

    def x_dev(step):
        return device((x + step + 4) % 4, y, z, c)

    row_peers = [(row + i) % 8 for i in range(1, 8)]
    sibling = row_dev((row + 4) % 8)

    local = [
        pltpu.make_async_copy(k, col.at[c, me, 0], lsem.at[0]),
        pltpu.make_async_copy(v, col.at[c, me, 1], lsem.at[1]),
        pltpu.make_async_copy(q_any, q, lsem.at[2]),
        pltpu.make_async_copy(d_any, d, lsem.at[3]),
        pltpu.make_async_copy(rand_any, rand, lsem.at[4]),
        pltpu.make_async_copy(glob_any, glob, lsem.at[5]),
    ]
    for cp in local:
        cp.start()
    greet(
        [
            device(x, (y + 1) % NY, z, c), device(x, (y + NY - 1) % NY, z, c),
            device(x, y, (z + 1) % NZ, c), device(x, y, (z + NZ - 1) % NZ, c),
        ]
        + [row_dev(r) for r in row_peers]
    )
    for cp in local:
        cp.wait()
    rand_copy = remote(rand_any, rand_sib, ssem.at[2], rsem.at[2], sibling)
    rand_copy.start()

    def pass_on(kv):
        def arrived(py, pz):
            ref = col.at[c, py * NZ + pz, kv]
            remote(ref, ref, ssem.at[3 + kv], rsem.at[3 + kv], sibling).start()

        return arrived

    def piece(kv):
        return lambda py, pz: col.at[c, py * NZ + pz, kv]

    def half(kv):
        return lambda py, pz, h: col.at[c, py * NZ + pz, kv, h]

    def some(kv):
        return col.at[0, pl.ds(0, PLANE - 1), kv]

    flow_k = gather_flow(
        piece(0), half(0), ("y", "z"), pos, c, (a_ssem, a_rsem), pass_on(0), 32, some(0)
    )
    flow_v = gather_flow(
        piece(1), half(1), ("z", "y"), pos, c, (b_ssem, b_rsem), pass_on(1), 32, some(1)
    )
    pass_on(0)(y, z)
    pass_on(1)(y, z)

    g_place = [place(glob[g]) for g in range(2)]
    shards = jnp.full((16, HD), shard, jnp.int32)
    for g in range(2):
        mine = shards == glob[g] // 2
        for t, ref in ((0, q), (1, d)):
            for p in range(PLANE):
                value = ref[g_place[g][3], p % 4, :, (p // 4) * HD : (p // 4 + 1) * HD]
                rows = slice((g * 2 + t) * 16, (g * 2 + t + 1) * 16)
                gown[p, rows, :] = jnp.where(mine, value, jnp.zeros_like(value))

    def tiles_done(value):
        sel[row] = value.reshape(2, 2, 16, HD).astype(BF16)

    flow_g = reduce_flow(
        lambda py, pz: gown.at[py * NZ + pz], g_got, g_out_buf, ("y", "z"), pos, c, (g_ssem, g_rsem),
        tiles_done, 16,
    )

    for j in range(2):
        for h in range(HEADS):
            rows = pl.ds(j * 512 + h * 64, 64)
            qs[rows, :] = q[j, :, :, h * HD : (h + 1) * HD].reshape(64, HD)
            ds_[rows, :] = d[j, :, :, h * HD : (h + 1) * HD].reshape(64, HD)

    play(flow_k, flow_v, flow_g)
    for r in row_peers:
        remote(sel.at[row], sel.at[row], ssem.at[6], rsem.at[6], row_dev(r)).start()

    for kv in range(2):
        remote(col.at[1 - c, :, kv], col.at[1 - c, :, kv], ssem.at[3 + kv], rsem.at[3 + kv], sibling).wait_recv()

    def wanted(ka_of, slot):
        if slot >= 6:
            return glob[slot - 6]
        return rand[slot % 3, ka_of * 2 + slot // 3]

    def ka_at(step):
        return zh * 4 + (x + step + 4) % 4

    def slot_at(direction, i):
        return i if direction == 0 else (i + 4) % 8

    for dr in range(2):
        for i in range(4):
            bx, bc, bp, bh = place(wanted(ka_at(2), slot_at(dr, i)))
            for kv in range(2):
                xs[dr, 9 + i, kv] = col[bc, bp, kv, bh]
    for dr in range(2):
        remote(
            xs.at[dr, pl.ds(9, 4)], xm.at[dr, 0], x_ssem.at[dr], x_rsem.at[dr], x_dev(1 - 2 * dr)
        ).start()
    for dr in range(2):
        step = 1 - 2 * dr
        for i in range(8):
            bx, bc, bp, bh = place(wanted(ka_at(step), slot_at(dr, i)))
            for kv in range(2):
                if i < 4:
                    xm[dr, 1, i, kv] = col[bc, bp, kv, bh]
                else:
                    xs[dr, i, kv] = col[bc, bp, kv, bh]
        to = pb * 8 + ka_at(step)
        edge = (to * 2 + 2 * SHARDS - 1) % NBLK if dr == 0 else (to * 2 + 2) % NBLK
        bx, bc, bp, bh = place(edge)
        for kv in range(2):
            xs[dr, 8, kv] = col[bc, bp, kv, bh]
        remote(
            xs.at[dr, pl.ds(4, 5)], xall.at[dr, pl.ds(4, 5)], x_ssem.at[2 + dr], x_rsem.at[2 + dr], x_dev(step)
        ).start()
    for slot in range(SLOTS):
        bx, bc, bp, bh = place(wanted(ka, slot))
        for kv in range(2):
            xall[2, slot, kv] = col[bc, bp, kv, bh]
    for dr in range(2):
        got = xm.at[dr, 0]
        remote(got, got, x_ssem.at[dr], x_rsem.at[dr], x_dev(1)).wait_recv()
    for dr in range(2):
        step = 1 - 2 * dr
        for i in range(4):
            bx = place(wanted(ka_at(step), slot_at(dr, i)))[0]
            which = jnp.where(bx == x, 1, 0)
            for kv in range(2):
                xs[dr, i, kv] = xm[dr, which, i, kv]
        remote(
            xs.at[dr, pl.ds(0, 4)], xall.at[dr, pl.ds(0, 4)], x_ssem.at[4 + dr], x_rsem.at[4 + dr], x_dev(step)
        ).start()

    remote(sel.at[pl.ds(0, 7)], sel.at[pl.ds(0, 7)], ssem.at[6], rsem.at[6], sibling).wait_recv()
    for g in range(2):
        gx, gc, gpl, gh = g_place[g]
        gq[pl.ds(g * 16, 16), :] = sel[gc * 4 + gx, g, 0]
        gd[pl.ds(g * 16, 16), :] = sel[gc * 4 + gx, g, 1]
    for i in range(4):
        lanes, ps = slice(i * 1024, (i + 1) * 1024), pl.ds(i * 8, 8)
        sg[:, lanes] = nt(gq[...], col[c, ps, 0].reshape(1024, HD)) * SCALE
        dpg[:, lanes] = nt(gd[...], col[c, ps, 1].reshape(1024, HD))
    g_max = jnp.max(sg[...], axis=1, keepdims=True)
    g_exp = jnp.exp(sg[...] - g_max)
    g_sum = jnp.sum(g_exp, axis=1, keepdims=True)
    g_dot = jnp.sum(g_exp * dpg[...], axis=1, keepdims=True)
    lane = lax.broadcasted_iota(jnp.int32, (32, HD), 1)
    stat[row] = jnp.where(lane == 0, g_max, jnp.where(lane == 1, g_sum, g_dot))
    for r in row_peers:
        remote(stat.at[row], stat.at[row], ssem.at[8], rsem.at[8], row_dev(r)).start()

    for dr in range(2):
        for lo, n, sem in ((4, 5, 2), (0, 4, 4)):
            ref = xall.at[dr, pl.ds(lo, n)]
            remote(ref, ref, x_ssem.at[sem + dr], x_rsem.at[sem + dr], x_dev(1)).wait_recv()
    slot_of = lax.broadcasted_iota(jnp.int32, (1, 512), 1) // BLOCK
    lo, hi = pl.ds(0, BLOCK), pl.ds(BLOCK, BLOCK)
    for j in range(2):
        block = shard * 2 + j
        cand = [block - 1, block, block + 1, glob[0], glob[1]]
        cand += [rand[r, ka * 2 + j] for r in range(3)]
        for kv, dst in ((0, kc), (1, vc)):
            near_refs = [xall.at[0, 8, kv], col.at[c, me, kv, 0], col.at[c, me, kv, 1], xall.at[1, 8, kv]]
            for i in range(3):
                dst[i * BLOCK : (i + 1) * BLOCK, :] = near_refs[i + j][...]
            for i in range(3, 8):
                slot = 6 + i - 3 if i < 5 else j * 3 + i - 5
                far = 0 if slot < 4 else 1
                off = (place(cand[i])[0] + 4 - x) % 4
                src = jnp.where(off == 0, 2, jnp.where(off == 3, 0, jnp.where(off == 1, 1, far)))
                spot = jnp.where(src == 1, (slot + 4) % 8, slot)
                dst[i * BLOCK : (i + 1) * BLOCK, :] = xall[src, spot, kv]
        cands = jnp.zeros((1, 512), jnp.int32)
        for i in range(8):
            cands = jnp.where(slot_of == i, cand[i], cands)
        out = (cands < 0) | (cands >= NBLK)
        for i in range(7):
            out = out | ((slot_of > i) & (cands == cand[i]))
        bias = jnp.where(out, NEG, 0.0)
        blocks = jnp.full((256, 1), block, jnp.int32)
        keep = jnp.where((blocks == glob[0]) | (blocks == glob[1]), 0.0, 1.0)
        for part_i in range(2):
            rows = pl.ds(j * 512 + part_i * 256, 256)
            qv, dv = qs[rows, :], ds_[rows, :]
            s = nt(qv, kc[...]) * SCALE + bias
            e = jnp.exp(s - jnp.max(s, axis=1, keepdims=True))
            w = e * (keep / jnp.sum(e, axis=1, keepdims=True))
            wb = w.astype(BF16)
            o = nn(wb, vc[...]).astype(BF16)
            dot = jnp.sum(dv.astype(F32) * o.astype(F32), axis=1, keepdims=True)
            ds = (w * (nt(dv, vc[...]) - dot)).astype(BF16)
            dqv = (nn(ds, kc[...]) * SCALE).astype(BF16)
            for h in range(4):
                cols = slice((part_i * 4 + h) * HD, (part_i * 4 + h + 1) * HD)
                att[j, :, :, cols] = o[h * 64 : (h + 1) * 64].reshape(4, 16, HD)
                dq[j, :, :, cols] = dqv[h * 64 : (h + 1) * 64].reshape(4, 16, HD)
            dk_new, dv_new = tn(ds, qv) * SCALE, tn(wb, dv)
            if part_i == 0:
                dkv[0], dkv[1] = dk_new, dv_new
            else:
                dkv[0] += dk_new
                dkv[1] += dv_new
        for kv in range(2):
            for i in range(8):
                term = dkv[kv, i * BLOCK : (i + 1) * BLOCK, :]
                spot = i + j - 1
                if i < 3 and spot in (-1, 2):
                    contrib[row, 9 if spot == -1 else 0, kv] = term.astype(BF16)
                elif i < 3:
                    if (j, i) in ((0, 1), (0, 2)):
                        own_sum[kv, pl.ds(spot * BLOCK, BLOCK), :] = term
                    else:
                        total = own_sum[kv, pl.ds(spot * BLOCK, BLOCK), :] + term
                        near_sum[kv, pl.ds(spot * BLOCK, BLOCK), :] = total
                elif i >= 5:
                    contrib[row, 1 + j * 3 + i - 5, kv] = term.astype(BF16)
                elif j == 0:
                    own_sum[2 + kv, pl.ds((i - 3) * BLOCK, BLOCK), :] = term
                else:
                    total = own_sum[2 + kv, pl.ds((i - 3) * BLOCK, BLOCK), :] + term
                    contrib[row, 7 + i - 3, kv] = total.astype(BF16)

    def c_copy(src, first, n, step, sem):
        ref = contrib.at[src, pl.ds(first, n)]
        dev = sibling if step is None else x_dev(step)
        return remote(ref, ref, c_ssem.at[sem], c_rsem.at[sem], dev)

    def at_x(o):
        return c * 4 + (x + o + 4) % 4

    c_sends = [c_copy(row, 0, 9, 1, 0), c_copy(row, 1, 9, -1, 1), c_copy(row, 1, 8, None, 4)]
    for cp in c_sends:
        cp.start()

    remote(stat.at[pl.ds(0, 7)], stat.at[pl.ds(0, 7)], ssem.at[8], rsem.at[8], sibling).wait_recv()
    stats = [stat[i] for i in range(8)]
    top = stats[0][:, 0:1]
    for i in range(1, 8):
        top = jnp.maximum(top, stats[i][:, 0:1])
    total, dot = jnp.zeros((32, 1), F32), jnp.zeros((32, 1), F32)
    for i in range(8):
        f = jnp.exp(stats[i][:, 0:1] - top)
        total += stats[i][:, 1:2] * f
        dot += stats[i][:, 2:3] * f
    g_row = lax.broadcasted_iota(jnp.int32, (32, 1), 0)
    g_one = jnp.full((32, 1), glob[1], jnp.int32)
    first = jnp.where((g_row >= 16) & (g_one == glob[0]), 0.0, 1.0)
    gw = jnp.exp(sg[...] - top) * (first / total)
    gp[...] = gw.astype(BF16)
    gs[...] = (gw * (dpg[...] - dot / total)).astype(BF16)
    g_o, g_dq = jnp.zeros((32, HD), F32), jnp.zeros((32, HD), F32)
    for i in range(4):
        lanes, ps = slice(i * 1024, (i + 1) * 1024), pl.ds(i * 8, 8)
        g_o += nn(gp[:, lanes], col[c, ps, 1].reshape(1024, HD))
        g_dq += nn(gs[:, lanes], col[c, ps, 0].reshape(1024, HD))
    part[row, 0] = g_o
    part[row, 1] = g_dq * SCALE
    for r in row_peers:
        remote(part.at[row], part.at[row], ssem.at[11], rsem.at[11], row_dev(r)).start()

    c_copy(at_x(-1), 0, 9, 1, 0).wait_recv()
    more = [c_copy(at_x(-1), 1, 4, 1, 2), c_copy(at_x(-1), 0, 9, None, 5)]
    for cp in more:
        cp.start()
    c_copy(at_x(1), 1, 9, -1, 1).wait_recv()
    more += [c_copy(at_x(1), 5, 4, -1, 3), c_copy(at_x(1), 1, 9, None, 6)]
    for cp in more[2:]:
        cp.start()
    c_sends += more

    for i in range(4):
        lanes, ps = slice(i * 1024, (i + 1) * 1024), pl.ds(i * 8, 8)
        dense[ps, 0] = (tn(gs[:, lanes], gq[...]) * SCALE).reshape(8, HD, HD)
        dense[ps, 1] = tn(gp[:, lanes], gd[...]).reshape(8, HD, HD)

    c_copy(at_x(2), 1, 4, 1, 2).wait_recv()
    c_copy(at_x(2), 5, 4, -1, 3).wait_recv()
    last = c_copy(at_x(2), 1, 8, None, 7)
    last.start()
    c_sends.append(last)

    remote(part.at[pl.ds(0, 7)], part.at[pl.ds(0, 7)], ssem.at[11], rsem.at[11], sibling).wait_recv()
    for t in range(2):
        acc = part[0, t]
        for i in range(1, 8):
            acc += part[i, t]
        for g in range(2):
            gout[t, g] = acc[g * 16 : (g + 1) * 16].astype(BF16)

    def at_other(o):
        return (1 - c) * 4 + (x + o + 4) % 4

    for sem, o, first, n in ((4, 0, 1, 8), (5, -1, 0, 9), (6, 1, 1, 9), (7, 2, 1, 8)):
        c_copy(at_other(o), first, n, None, sem).wait_recv()
    rand_copy.wait_recv()

    for cp in c_sends + [rand_copy]:
        cp.wait_send()
    for kv in range(2):
        remote(col.at[c, :, kv], col.at[c, :, kv], ssem.at[3 + kv], rsem.at[3 + kv], sibling).wait_send()
    for ref, sem in ((sel, 6), (stat, 8), (part, 11)):
        remote(ref.at[pl.ds(0, 7)], ref.at[pl.ds(0, 7)], ssem.at[sem], rsem.at[sem], sibling).wait_send()
    for dr in range(2):
        for first, n, sem in ((9, 4, 0), (4, 5, 2), (0, 4, 4)):
            ref = xs.at[dr, pl.ds(first, n)]
            remote(ref, ref, x_ssem.at[sem + dr], x_rsem.at[sem + dr], x_dev(1)).wait_send()


def kernel_b(rand, rand_sib, glob, contrib, dense, acc):
    x, y, z, c = here()
    zh = z // 4
    del dense

    def add(block, here_too, src, entry):
        bx, bc, bp, bh = place(block)

        @pl.when(here_too & (bx == x) & (bc == c))
        def _():
            rows = pl.ds(pl.multiple_of(bh * BLOCK, BLOCK), BLOCK)
            acc[bp, :, rows, :] += contrib[src, entry].astype(F32)

    for core in range(2):
        for xs in range(NX):
            src = core * 4 + xs
            shard = ((y * 4 + z % 4) * 2 + core) * 8 + zh * 4 + xs
            for slot in range(SLOTS):
                if slot >= 6:
                    block = glob[slot - 6]
                else:
                    r, s = (zh * 4 + xs) * 2 + slot // 3, slot % 3
                    block = jnp.where(c == core, rand[s, r], rand_sib[s, r])
                add(block, True, src, 1 + slot)
            after, before = shard * 2 + 2, shard * 2 - 1
            add(jnp.minimum(after, NBLK - 1), (after < NBLK) & ((xs - x + 4) % 4 == 3), src, 0)
            add(jnp.maximum(before, 0), (before >= 0) & ((xs - x + 4) % 4 == 1), src, 9)


def kernel_c(
    acc, gout,
    sums, gall,
    got_k, out_k, got_v, out_v,
    k_ssem, k_rsem, v_ssem, v_rsem, o_ssem, o_rsem, w_ssem, w_rsem, lsem,
):
    x, y, z, c = here()
    me = y * NZ + z
    own = pltpu.make_async_copy(gout, gall.at[me], lsem.at[0])
    own.start()
    greet(
        [
            device(x, (y + 1) % NY, z, c), device(x, (y + NY - 1) % NY, z, c),
            device(x, y, (z + 1) % NZ, c), device(x, y, (z + NZ - 1) % NZ, c),
        ]
    )
    own.wait()
    pos = (x, y, z)

    def finish(kv):
        def done(value):
            sums[kv] = value

        return done

    def term(kv):
        return lambda py, pz: acc.at[py * NZ + pz, kv]

    def piece(t):
        return lambda py, pz: gall.at[py * NZ + pz, t]

    def half(t):
        return lambda py, pz, h: gall.at[py * NZ + pz, t, h]

    nothing = lambda py, pz: None
    some = [gall.at[pl.ds(0, PLANE - 1), t] for t in range(2)]
    play(
        reduce_flow(term(0), got_k, out_k, ("z", "y"), pos, c, (k_ssem, k_rsem), finish(0), 32),
        reduce_flow(term(1), got_v, out_v, ("y", "z"), pos, c, (v_ssem, v_rsem), finish(1), 32),
        gather_flow(piece(0), half(0), ("y", "z"), pos, c, (o_ssem, o_rsem), nothing, 8, some[0]),
        gather_flow(piece(1), half(1), ("z", "y"), pos, c, (w_ssem, w_rsem), nothing, 8, some[1]),
    )


def kernel_d(glob, sums, near_sum, att_in, dq_in, gall, att, dq, dk, dv):
    shard = lax.axis_index("pb") * 8 + lax.axis_index("ka")
    dk[...] = (sums[0] + near_sum[0]).astype(BF16)
    dv[...] = (sums[1] + near_sum[1]).astype(BF16)
    for j in range(2):
        blocks = jnp.full((16, HD), shard * 2 + j, jnp.int32)
        is_glob = [blocks == glob[g] for g in range(2)]
        for t, src, dst in ((0, att_in, att), (1, dq_in, dq)):
            for p in range(PLANE):
                cols = slice((p // 4) * HD, (p // 4 + 1) * HD)
                value = jnp.where(is_glob[1], gall[p, t, 1], src[j, p % 4, :, cols])
                dst[j, p % 4, :, cols] = jnp.where(is_glob[0], gall[p, t, 0], value)


def body(queries, key_vectors, value_vectors, out_grad, rand_blocks, global_blocks):
    vmem = pl.BlockSpec(memory_space=pltpu.VMEM)
    smem = pl.BlockSpec(memory_space=pltpu.SMEM)
    hbm = pl.BlockSpec(memory_space=pl.ANY)
    off = pl.BlockSpec(memory_space=pltpu.HBM)
    shape = jax.ShapeDtypeStruct
    dma = pltpu.SemaphoreType.DMA
    rows = (2, 4, 16, HEADS * HD)
    rand = rand_blocks.T
    yz, zy = ("y", "z"), ("z", "y")
    ga, gb = GATHER_SEMS[yz], GATHER_SEMS[zy]
    mk, mv = REDUCE_MSGS[zy], REDUCE_MSGS[yz]
    att, dq, contrib, dense, near_sum, gout, rand_sib = pl.pallas_call(
        kernel_a,
        name="exchange_and_attend",
        out_shape=(
            shape(rows, BF16),
            shape(rows, BF16),
            shape((8, SLOTS + 2, 2, BLOCK, HD), BF16),
            shape((PLANE, 2, HD, HD), F32),
            shape((2, HD, HD), F32),
            shape((2, 2, 16, HD), BF16),
            shape((3, 16), jnp.int32),
        ),
        in_specs=[off] * 6,
        out_specs=(vmem, vmem, vmem, vmem, vmem, vmem, hbm),
        scratch_shapes=[
            pltpu.VMEM((2, PLANE, 2, 2, BLOCK, HD), BF16),
            pltpu.VMEM((PLANE, 64, HD), BF16),
            pltpu.VMEM((mv, 64, HD), BF16),
            pltpu.VMEM((mv, 64, HD), BF16),
            pltpu.VMEM((8, 2, 2, 16, HD), BF16),
            pltpu.VMEM((2, 2, 4, 2, BLOCK, HD), BF16),
            pltpu.VMEM((2, 13, 2, BLOCK, HD), BF16),
            pltpu.VMEM((3, 9, 2, BLOCK, HD), BF16),
            pltpu.VMEM((8, 32, HD), F32),
            pltpu.VMEM((8, 2, 32, HD), F32),
            pltpu.SMEM((3, 16), jnp.int32),
            pltpu.SMEM((2,), jnp.int32),
            pltpu.VMEM(rows, BF16),
            pltpu.VMEM(rows, BF16),
            pltpu.VMEM((32, PLANE * HD), F32),
            pltpu.VMEM((32, PLANE * HD), F32),
            pltpu.VMEM((32, PLANE * HD), BF16),
            pltpu.VMEM((32, PLANE * HD), BF16),
            pltpu.VMEM((32, HD), BF16),
            pltpu.VMEM((32, HD), BF16),
            pltpu.VMEM((512, HD), BF16),
            pltpu.VMEM((512, HD), BF16),
            pltpu.VMEM((1024, HD), BF16),
            pltpu.VMEM((1024, HD), BF16),
            pltpu.VMEM((2, 512, HD), F32),
            pltpu.VMEM((4, HD, HD), F32),
            dma((1,)), dma((ga,)), dma((1,)), dma((gb,)), dma((1,)), dma((mv,)),
            dma((8,)), dma((8,)), dma((6,)), dma((6,)), dma((12,)), dma((12,)), dma((6,)),
        ],
        compiler_params=pltpu.CompilerParams(
            collective_id=0, has_side_effects=True, vmem_limit_bytes=VMEM_A
        ),
    )(
        rand, global_blocks, queries.reshape(rows),
        key_vectors.reshape(2, BLOCK, HD), value_vectors.reshape(2, BLOCK, HD), out_grad.reshape(rows),
    )
    acc = pl.pallas_call(
        kernel_b,
        name="spread_terms",
        out_shape=shape((PLANE, 2, HD, HD), F32),
        in_specs=[smem, smem, smem, vmem, vmem],
        out_specs=vmem,
        input_output_aliases={4: 0},
        compiler_params=pltpu.CompilerParams(vmem_limit_bytes=VMEM_B),
    )(rand, rand_sib, global_blocks, contrib, dense)
    sums, gall = pl.pallas_call(
        kernel_c,
        name="reduce_and_gather",
        out_shape=(shape((2, HD, HD), F32), shape((PLANE, 2, 2, 16, HD), BF16)),
        in_specs=[vmem] * 2,
        out_specs=(vmem,) * 2,
        scratch_shapes=[
            pltpu.VMEM((mk, HD, HD), BF16), pltpu.VMEM((mk, HD, HD), BF16),
            pltpu.VMEM((mv, HD, HD), BF16), pltpu.VMEM((mv, HD, HD), BF16),
            dma((1,)), dma((mk,)), dma((1,)), dma((mv,)),
            dma((1,)), dma((ga,)), dma((1,)), dma((gb,)), dma((1,)),
        ],
        compiler_params=pltpu.CompilerParams(
            collective_id=1, has_side_effects=True, vmem_limit_bytes=VMEM_C
        ),
    )(acc, gout)
    att, dq, dk, dv = pl.pallas_call(
        kernel_d,
        name="finish",
        out_shape=(shape(rows, BF16), shape(rows, BF16), shape((HD, HD), BF16), shape((HD, HD), BF16)),
        in_specs=[smem] + [vmem] * 5,
        out_specs=(vmem,) * 4,
        compiler_params=pltpu.CompilerParams(vmem_limit_bytes=VMEM_D),
    )(global_blocks, sums, near_sum, att, dq, gall)
    return att.reshape(queries.shape), dq.reshape(queries.shape), dk, dv


def solution(mesh):
    assert (mesh.shape["pb"], mesh.shape["ka"]) == (32, 8)
    rows = P(("pb", "ka"), None)
    return jax.shard_map(
        body,
        mesh=mesh,
        in_specs=(rows, rows, rows, rows, P("pb", None), P()),
        out_specs=(rows, rows, rows, rows),
        check_vma=False,
    )
```

time: 142 us -> 107 us (0.75)
  Pallas kernels: 132 us -> 101 us
  local copies, waits for them, and re-layouts: 7.44 us -> 4.74 us
    pallas_call x2 -> x3, Pallas kernels: 120 us -> 97.4 us  [the longest x1 66 us: body(): pl.pallas_call(kernel_a, name='exchange_and_attend', out_shape=(shape(row...]
    pallas_call x1, Pallas kernels: 12.5 us -> 3.58 us  [body(): pl.pallas_call(kernel_b, name='spread_terms', out_shape=shape((PLANE, 2,...]
    unnamed x5 -> x12, local copies, waits for them, and re-layouts: 7.44 us -> 4.74 us
where the time goes in v2:
time: 107 us; the launch traced here: 106 us
  Pallas kernels  101 us (94%)
  local copies, waits for them, and re-layouts  4.74 us (4%)
    pallas_call x1, Pallas kernels, body(): pl.pallas_call(kernel_a, name='exchange_and_attend', out_shape=(shape(row...  66 us
    pallas_call x1, Pallas kernels, body(): pl.pallas_call(kernel_c, name='reduce_and_gather', out_shape=(shape((2, H...  29.9 us
    unnamed x12, local copies, waits for them, and re-layouts  4.74 us
    pallas_call x1, Pallas kernels, body(): pl.pallas_call(kernel_b, name='spread_terms', out_shape=shape((PLANE, 2,...  3.58 us

profile of v2, /device:TPU:2, one launch (start us, length us, event | category | flops | bytes accessed | tf_op | source)
XLA Modules:
  0.0 106.4 jit_solution(14302466767902003898)
XLA Ops:
  0.6 0.0 copy-start
  0.6 0.9 copy-done
  1.6 0.0 copy-start.1
  1.6 0.9 copy-done.1
  2.5 0.0 copy-start.2
  2.5 0.8 copy-done.2
  3.3 0.0 copy-start.3
  3.3 0.8 copy-done.3
  4.1 0.0 copy-start.4
  4.1 0.7 copy-done.4
  4.7 0.0 copy-start.5
  4.7 0.7 copy-done.5
  5.4 66.0 %exchange_and_attend.1 = (bf16[2,4,16,1024]{3,2,1,0:T(8,128)(2,1)S(1)}, bf16[2,4,16,1024]{3,2,1,0:T(8,128)(2,1)S(1)}, bf16[8,10,2,64,128]{4,3,2,1,0:T(8,128)(2,1...) custom-call(s32[3,16]{1,0:T(4,128)S(1)} %bitcast.11, ...), custom_call_target="tpu_custom_call" | custom-call | tf_op jit(solution)/shard_map/exchange_and_attend/pallas_call | solution.py:684
  71.4 3.6 %spread_terms.1.acc = f32[32,2,128,128]{3,2,1,0:T(8,128)S(1)} custom-call(s32[3,16]{1,0:T(4,128)S(1)} %bitcast.12, s32[3,16]{1,0:T(4,128)S(1)} %get-tuple-element.17.rand_sib, s32[2]{0:T(128)S(1)} %copy-done.5, bf16[8,10,2,64,128]{4,3,2,1,0:T(8,128)(2,1)S(1)} %get-tuple-element.18.contrib, ...), custom_call_target="tpu_custom_call", output_to_operand_aliasing={{}: (4, {})} | custom-call | tf_op jit(solution)/shard_map/spread_terms/pallas_call | solution.py:735
  75.0 29.9 %reduce_and_gather.1 = (f32[2,128,128]{2,1,0:T(8,128)S(1)}, bf16[32,2,2,16,128]{4,3,2,1,0:T(8,128)(2,1)S(1)}) custom-call(f32[32,2,128,128]{3,2,1,0:T(8,128)S(1)} %spread_terms.1.acc, bf16[2,2,16,128]{3,2,1,0:T(8,128)(2,1)S(1)} %get-tuple-element.20.gout), custom_call_target="tpu_custom_call" | custom-call | tf_op jit(solution)/shard_map/reduce_and_gather/pallas_call | solution.py:744
  104.9 1.6 %finish.1 = (bf16[2,4,16,1024]{3,2,1,0:T(8,128)(2,1)}, bf16[2,4,16,1024]{3,2,1,0:T(8,128)(2,1)}, bf16[128,128]{1,0:T(8,128)(2,1)}, bf16[128,128]{1,0:T(8,128)(2,1)}) custom-call(s32[2]{0:T(128)S(1)} %copy-done.5, f32[2,128,128]{2,1,0:T(8,128)S(1)} %get-tuple-element.21.sums, f32[2,128,128]{2,1,0:T(8,128)S(1)} %get-tuple-element.22.near_sum, ...), custom_call_target="tpu_custom_call" | custom-call | tf_op jit(solution)/shard_map/finish/pallas_call | solution.py:760
Async XLA Ops:
  0.6 1.0 copy-start
  1.6 0.9 copy-start.1
  2.5 0.8 copy-start.2
  3.3 0.8 copy-start.3
  4.1 0.7 copy-start.4
  4.7 0.7 copy-start.5

commit v3 on v2

--- a/solution.py
+++ b/solution.py
@@ -43,25 +43,31 @@
     )
 
 
-RATE, LATENCY, AHEAD = 37.0, 1.6, 2.0
-
-
-def schedule(msgs):
-    depth = [1] * len(msgs)
-    for i in range(len(msgs) - 1, -1, -1):
-        for dep in msgs[i][0]:
-            depth[dep] = max(depth[dep], depth[i] + 1)
-    ranked = sorted(range(len(msgs)), key=lambda i: (-depth[i], i))
+RATE, CORE_RATE, LATENCY, AHEAD, FAVOUR = 50.0, 200.0, 1.6, 2.0, 0
+
+
+def schedule(msgs, favoured=()):
+    depth, changed = [1] * len(msgs), True
+    while changed:
+        changed = False
+        for i in range(len(msgs) - 1, -1, -1):
+            for dep in msgs[i][0]:
+                if depth[dep] <= depth[i]:
+                    depth[dep], changed = depth[i] + 1, True
+    ranked = sorted(range(len(msgs)), key=lambda i: (-depth[i] - (FAVOUR if i in favoured else 0), i))
     now, free, arrival, come, order = 0.0, {}, {}, set(), []
     while len(come) < len(msgs):
         for i in ranked:
             deps, link, size, work = msgs[i][:4]
-            begin = max(free.get(link, 0.0), now)
+            begin = now if link is None else max(free.get(link, 0.0), now)
             if i in arrival or begin > now + AHEAD or any(dep not in come for dep in deps):
                 continue
             now += work
-            free[link] = max(begin, now) + size / RATE
-            arrival[i] = free[link] + LATENCY
+            if link is None:
+                arrival[i] = now + size
+            else:
+                free[link] = max(begin, now) + size / (CORE_RATE if link == "core" else RATE)
+                arrival[i] = free[link] + LATENCY
             order.append(("send", i))
         i = min((i for i in arrival if i not in come), key=lambda i: (arrival[i], i))
         now = max(now, arrival[i]) + 0.05
@@ -70,12 +76,18 @@
     return order
 
 
-def play(*flows):
-    msgs = []
+def play(flows, more=None, after=None, favour=None):
+    msgs, members = [], []
     for own, end in flows:
         base = len(msgs)
+        members.append(list(range(base, base + len(own))))
         msgs += [([dep + base for dep in m[0]],) + m[1:] for m in own]
-    for what, i in schedule(msgs):
+    first = len(msgs)
+    if after is not None:
+        msgs = [(m[0] or after(first),) + m[1:] for m in msgs]
+    if more is not None:
+        msgs += more(members)
+    for what, i in schedule(msgs, () if favour is None else members[favour]):
         msgs[i][4 if what == "send" else 5]()
     for own, end in flows:
         end()
@@ -219,13 +231,17 @@
 
     base = ring(n2, order[1], term2, lambda o: ends[o])
 
+    def result():
+        last = (base + n2 // 2 - 1, base + n2 - 1)
+        return term2(0)(None) + load(got.at[last[0]], None) + load(got.at[last[1]], None)
+
     def end():
-        last = (base + n2 // 2 - 1, base + n2 - 1)
-        done(term2(0)(None) + load(got.at[last[0]], None) + load(got.at[last[1]], None))
+        if done is not None:
+            done(result())
         whole = out.at[pl.ds(0, PLANE - 1)]
         remote(whole, whole, ssem.at[0], rsem.at[0], dev("y", 0)).wait_send()
 
-    return msgs, end
+    return (msgs, end), result
 
 
 REDUCE_MSGS = {("y", "z"): NY * NZ + NZ, ("z", "y"): NZ * NY + NY}
@@ -253,11 +269,12 @@
 def kernel_a(
     rand_any, glob_any, q_any, k, v, d_any,
     att, dq, contrib, dense, near_sum, gout, rand_sib,
-    col, gown, g_got, g_out_buf, sel, xm, xs, xall, stat, part,
+    col_k, col_v, gown, g_got, g_out_buf, sel, xm_a, xm_b, xm_c, xm_d, xs, xall, stat, part,
     rand, glob, q, d, sg, dpg, gp, gs, gq, gd, kc, vc, qs, ds_, dkv, own_sum,
     a_ssem, a_rsem, b_ssem, b_rsem, g_ssem, g_rsem, c_ssem, c_rsem, x_ssem, x_rsem, ssem, rsem, lsem,
 ):
     x, y, z, c = here()
+    col, xm = (col_k, col_v), ((xm_a, xm_b), (xm_c, xm_d))
     pb, ka = lax.axis_index("pb"), lax.axis_index("ka")
     shard = pb * 8 + ka
     me = y * NZ + z
@@ -275,8 +292,8 @@
     sibling = row_dev((row + 4) % 8)
 
     local = [
-        pltpu.make_async_copy(k, col.at[c, me, 0], lsem.at[0]),
-        pltpu.make_async_copy(v, col.at[c, me, 1], lsem.at[1]),
+        pltpu.make_async_copy(k, col[0].at[c, me], lsem.at[0]),
+        pltpu.make_async_copy(v, col[1].at[c, me], lsem.at[1]),
         pltpu.make_async_copy(q_any, q, lsem.at[2]),
         pltpu.make_async_copy(d_any, d, lsem.at[3]),
         pltpu.make_async_copy(rand_any, rand, lsem.at[4]),
@@ -298,19 +315,19 @@
 
     def pass_on(kv):
         def arrived(py, pz):
-            ref = col.at[c, py * NZ + pz, kv]
+            ref = col[kv].at[c, py * NZ + pz]
             remote(ref, ref, ssem.at[3 + kv], rsem.at[3 + kv], sibling).start()
 
         return arrived
 
     def piece(kv):
-        return lambda py, pz: col.at[c, py * NZ + pz, kv]
+        return lambda py, pz: col[kv].at[c, py * NZ + pz]
 
     def half(kv):
-        return lambda py, pz, h: col.at[c, py * NZ + pz, kv, h]
+        return lambda py, pz, h: col[kv].at[c, py * NZ + pz, h]
 
     def some(kv):
-        return col.at[0, pl.ds(0, PLANE - 1), kv]
+        return col[kv].at[0, pl.ds(0, PLANE - 1)]
 
     flow_k = gather_flow(
         piece(0), half(0), ("y", "z"), pos, c, (a_ssem, a_rsem), pass_on(0), 32, some(0)
@@ -331,12 +348,9 @@
                 rows = slice((g * 2 + t) * 16, (g * 2 + t + 1) * 16)
                 gown[p, rows, :] = jnp.where(mine, value, jnp.zeros_like(value))
 
-    def tiles_done(value):
-        sel[row] = value.reshape(2, 2, 16, HD).astype(BF16)
-
-    flow_g = reduce_flow(
+    flow_g, tiles = reduce_flow(
         lambda py, pz: gown.at[py * NZ + pz], g_got, g_out_buf, ("y", "z"), pos, c, (g_ssem, g_rsem),
-        tiles_done, 16,
+        None, 16,
     )
 
     for j in range(2):
@@ -345,12 +359,13 @@
             qs[rows, :] = q[j, :, :, h * HD : (h + 1) * HD].reshape(64, HD)
             ds_[rows, :] = d[j, :, :, h * HD : (h + 1) * HD].reshape(64, HD)
 
-    play(flow_k, flow_v, flow_g)
-    for r in row_peers:
-        remote(sel.at[row], sel.at[row], ssem.at[6], rsem.at[6], row_dev(r)).start()
-
-    for kv in range(2):
-        remote(col.at[1 - c, :, kv], col.at[1 - c, :, kv], ssem.at[3 + kv], rsem.at[3 + kv], sibling).wait_recv()
+    def send_sel():
+        sel[row] = tiles().reshape(2, 2, 16, HD).astype(BF16)
+        for r in row_peers:
+            remote(sel.at[row], sel.at[row], ssem.at[6], rsem.at[6], row_dev(r)).start()
+
+    def wait_sel():
+        remote(sel.at[pl.ds(0, 7)], sel.at[pl.ds(0, 7)], ssem.at[6], rsem.at[6], sibling).wait_recv()
 
     def wanted(ka_of, slot):
         if slot >= 6:
@@ -363,80 +378,100 @@
     def slot_at(direction, i):
         return i if direction == 0 else (i + 4) % 8
 
-    for dr in range(2):
+    def block_of(kv, block):
+        bx, bc, bp, bh = place(block)
+        return col[kv][bc, bp, bh]
+
+    def x_copy(kv, dr, kind):
+        src, dst = (
+            (xs.at[kv, dr, pl.ds(9, 4)], xm[kv][dr].at[0]),
+            (xs.at[kv, dr, pl.ds(4, 5)], xall.at[kv, dr, pl.ds(4, 5)]),
+            (xs.at[kv, dr, pl.ds(0, 4)], xall.at[kv, dr, pl.ds(0, 4)]),
+        )[kind]
+        sem = kv * 6 + dr * 3 + kind
+        return remote(src, dst, x_ssem.at[sem], x_rsem.at[sem], x_dev(1 - 2 * dr))
+
+    def column_in(kv):
+        ref = col[kv].at[1 - c]
+        remote(ref, ref, ssem.at[3 + kv], rsem.at[3 + kv], sibling).wait_recv()
+
+    def send_far(kv, dr):
         for i in range(4):
-            bx, bc, bp, bh = place(wanted(ka_at(2), slot_at(dr, i)))
-            for kv in range(2):
-                xs[dr, 9 + i, kv] = col[bc, bp, kv, bh]
-    for dr in range(2):
-        remote(
-            xs.at[dr, pl.ds(9, 4)], xm.at[dr, 0], x_ssem.at[dr], x_rsem.at[dr], x_dev(1 - 2 * dr)
-        ).start()
-    for dr in range(2):
+            xs[kv, dr, 9 + i] = block_of(kv, wanted(ka_at(2), slot_at(dr, i)))
+        x_copy(kv, dr, 0).start()
+
+    def send_near(kv, dr):
         step = 1 - 2 * dr
-        for i in range(8):
-            bx, bc, bp, bh = place(wanted(ka_at(step), slot_at(dr, i)))
-            for kv in range(2):
-                if i < 4:
-                    xm[dr, 1, i, kv] = col[bc, bp, kv, bh]
-                else:
-                    xs[dr, i, kv] = col[bc, bp, kv, bh]
+        for i in range(4, 8):
+            xs[kv, dr, i] = block_of(kv, wanted(ka_at(step), slot_at(dr, i)))
         to = pb * 8 + ka_at(step)
         edge = (to * 2 + 2 * SHARDS - 1) % NBLK if dr == 0 else (to * 2 + 2) % NBLK
-        bx, bc, bp, bh = place(edge)
-        for kv in range(2):
-            xs[dr, 8, kv] = col[bc, bp, kv, bh]
-        remote(
-            xs.at[dr, pl.ds(4, 5)], xall.at[dr, pl.ds(4, 5)], x_ssem.at[2 + dr], x_rsem.at[2 + dr], x_dev(step)
-        ).start()
-    for slot in range(SLOTS):
-        bx, bc, bp, bh = place(wanted(ka, slot))
-        for kv in range(2):
-            xall[2, slot, kv] = col[bc, bp, kv, bh]
-    for dr in range(2):
-        got = xm.at[dr, 0]
-        remote(got, got, x_ssem.at[dr], x_rsem.at[dr], x_dev(1)).wait_recv()
-    for dr in range(2):
-        step = 1 - 2 * dr
+        xs[kv, dr, 8] = block_of(kv, edge)
+        x_copy(kv, dr, 1).start()
         for i in range(4):
-            bx = place(wanted(ka_at(step), slot_at(dr, i)))[0]
-            which = jnp.where(bx == x, 1, 0)
-            for kv in range(2):
-                xs[dr, i, kv] = xm[dr, which, i, kv]
-        remote(
-            xs.at[dr, pl.ds(0, 4)], xall.at[dr, pl.ds(0, 4)], x_ssem.at[4 + dr], x_rsem.at[4 + dr], x_dev(step)
-        ).start()
-
-    remote(sel.at[pl.ds(0, 7)], sel.at[pl.ds(0, 7)], ssem.at[6], rsem.at[6], sibling).wait_recv()
-    for g in range(2):
-        gx, gc, gpl, gh = g_place[g]
-        gq[pl.ds(g * 16, 16), :] = sel[gc * 4 + gx, g, 0]
-        gd[pl.ds(g * 16, 16), :] = sel[gc * 4 + gx, g, 1]
-    for i in range(4):
-        lanes, ps = slice(i * 1024, (i + 1) * 1024), pl.ds(i * 8, 8)
-        sg[:, lanes] = nt(gq[...], col[c, ps, 0].reshape(1024, HD)) * SCALE
-        dpg[:, lanes] = nt(gd[...], col[c, ps, 1].reshape(1024, HD))
-    g_max = jnp.max(sg[...], axis=1, keepdims=True)
-    g_exp = jnp.exp(sg[...] - g_max)
-    g_sum = jnp.sum(g_exp, axis=1, keepdims=True)
-    g_dot = jnp.sum(g_exp * dpg[...], axis=1, keepdims=True)
-    lane = lax.broadcasted_iota(jnp.int32, (32, HD), 1)
-    stat[row] = jnp.where(lane == 0, g_max, jnp.where(lane == 1, g_sum, g_dot))
-    for r in row_peers:
-        remote(stat.at[row], stat.at[row], ssem.at[8], rsem.at[8], row_dev(r)).start()
-
-    for dr in range(2):
-        for lo, n, sem in ((4, 5, 2), (0, 4, 4)):
-            ref = xall.at[dr, pl.ds(lo, n)]
-            remote(ref, ref, x_ssem.at[sem + dr], x_rsem.at[sem + dr], x_dev(1)).wait_recv()
+            xm[kv][dr][1, i] = block_of(kv, wanted(ka_at(step), slot_at(dr, i)))
+        for i in range(4):
+            xall[kv, 2, dr * 4 + i] = block_of(kv, wanted(ka, dr * 4 + i))
+
+    def send_merged(kv, dr):
+        for i in range(4):
+            bx = place(wanted(ka_at(1 - 2 * dr), slot_at(dr, i)))[0]
+            xs[kv, dr, i] = xm[kv][dr][jnp.where(bx == x, 1, 0), i]
+        x_copy(kv, dr, 2).start()
+
+    def global_scores():
+        for g in range(2):
+            gx, gc, gpl, gh = g_place[g]
+            gq[pl.ds(g * 16, 16), :] = sel[gc * 4 + gx, g, 0]
+            gd[pl.ds(g * 16, 16), :] = sel[gc * 4 + gx, g, 1]
+        for i in range(4):
+            lanes, ps = slice(i * 1024, (i + 1) * 1024), pl.ds(i * 8, 8)
+            sg[:, lanes] = nt(gq[...], col[0][c, ps].reshape(1024, HD)) * SCALE
+            dpg[:, lanes] = nt(gd[...], col[1][c, ps].reshape(1024, HD))
+        g_max = jnp.max(sg[...], axis=1, keepdims=True)
+        g_exp = jnp.exp(sg[...] - g_max)
+        g_sum = jnp.sum(g_exp, axis=1, keepdims=True)
+        g_dot = jnp.sum(g_exp * dpg[...], axis=1, keepdims=True)
+        lane = lax.broadcasted_iota(jnp.int32, (32, HD), 1)
+        stat[row] = jnp.where(lane == 0, g_max, jnp.where(lane == 1, g_sum, g_dot))
+        for r in row_peers:
+            remote(stat.at[row], stat.at[row], ssem.at[8], rsem.at[8], row_dev(r)).start()
+
+    nothing = lambda: None
+
+    def exchange(members):
+        keys, values, rows_g = members
+        n = len(keys) + len(values) + len(rows_g)
+        more = [(rows_g, None, 2.5, 0.1, send_sel, wait_sel)]
+        for kv, flow in ((0, keys), (1, values)):
+            here_in = n + len(more)
+            more.append((flow, None, 1.6, 0.0, nothing, lambda kv=kv: column_in(kv)))
+            far = n + len(more)
+            for kind, send, deps, kb in (
+                (0, send_far, lambda dr: [here_in], 64),
+                (1, send_near, lambda dr: [here_in], 80),
+                (2, send_merged, lambda dr: [here_in, far + dr, far + 2 + dr], 64),
+            ):
+                for dr in range(2):
+                    more.append(
+                        (
+                            deps(dr), ("x", dr), kb, 0.2,
+                            lambda kv=kv, dr=dr, send=send: send(kv, dr),
+                            lambda kv=kv, dr=dr, kind=kind: x_copy(kv, dr, kind).wait_recv(),
+                        )
+                    )
+        more.append((keys + values + [n], None, 0.1, 1.5, global_scores, nothing))
+        return more
+
+    play((flow_k, flow_v, flow_g), exchange, favour=0)
+
     slot_of = lax.broadcasted_iota(jnp.int32, (1, 512), 1) // BLOCK
-    lo, hi = pl.ds(0, BLOCK), pl.ds(BLOCK, BLOCK)
     for j in range(2):
         block = shard * 2 + j
         cand = [block - 1, block, block + 1, glob[0], glob[1]]
         cand += [rand[r, ka * 2 + j] for r in range(3)]
         for kv, dst in ((0, kc), (1, vc)):
-            near_refs = [xall.at[0, 8, kv], col.at[c, me, kv, 0], col.at[c, me, kv, 1], xall.at[1, 8, kv]]
+            near_refs = [xall.at[kv, 0, 8], col[kv].at[c, me, 0], col[kv].at[c, me, 1], xall.at[kv, 1, 8]]
             for i in range(3):
                 dst[i * BLOCK : (i + 1) * BLOCK, :] = near_refs[i + j][...]
             for i in range(3, 8):
@@ -445,7 +480,7 @@
                 off = (place(cand[i])[0] + 4 - x) % 4
                 src = jnp.where(off == 0, 2, jnp.where(off == 3, 0, jnp.where(off == 1, 1, far)))
                 spot = jnp.where(src == 1, (slot + 4) % 8, slot)
-                dst[i * BLOCK : (i + 1) * BLOCK, :] = xall[src, spot, kv]
+                dst[i * BLOCK : (i + 1) * BLOCK, :] = xall[kv, src, spot]
         cands = jnp.zeros((1, 512), jnp.int32)
         for i in range(8):
             cands = jnp.where(slot_of == i, cand[i], cands)
@@ -527,8 +562,8 @@
     g_o, g_dq = jnp.zeros((32, HD), F32), jnp.zeros((32, HD), F32)
     for i in range(4):
         lanes, ps = slice(i * 1024, (i + 1) * 1024), pl.ds(i * 8, 8)
-        g_o += nn(gp[:, lanes], col[c, ps, 1].reshape(1024, HD))
-        g_dq += nn(gs[:, lanes], col[c, ps, 0].reshape(1024, HD))
+        g_o += nn(gp[:, lanes], col[1][c, ps].reshape(1024, HD))
+        g_dq += nn(gs[:, lanes], col[0][c, ps].reshape(1024, HD))
     part[row, 0] = g_o
     part[row, 1] = g_dq * SCALE
     for r in row_peers:
@@ -573,19 +608,27 @@
     for cp in c_sends + [rand_copy]:
         cp.wait_send()
     for kv in range(2):
-        remote(col.at[c, :, kv], col.at[c, :, kv], ssem.at[3 + kv], rsem.at[3 + kv], sibling).wait_send()
+        remote(col[kv].at[c], col[kv].at[c], ssem.at[3 + kv], rsem.at[3 + kv], sibling).wait_send()
     for ref, sem in ((sel, 6), (stat, 8), (part, 11)):
         remote(ref.at[pl.ds(0, 7)], ref.at[pl.ds(0, 7)], ssem.at[sem], rsem.at[sem], sibling).wait_send()
-    for dr in range(2):
-        for first, n, sem in ((9, 4, 0), (4, 5, 2), (0, 4, 4)):
-            ref = xs.at[dr, pl.ds(first, n)]
-            remote(ref, ref, x_ssem.at[sem + dr], x_rsem.at[sem + dr], x_dev(1)).wait_send()
-
-
-def kernel_b(rand, rand_sib, glob, contrib, dense, acc):
+    for kv in range(2):
+        for dr in range(2):
+            for kind in range(3):
+                x_copy(kv, dr, kind).wait_send()
+
+
+def kernel_b(rand_any, rand_sib, glob_any, contrib, dense, acc, rand, glob, sem):
     x, y, z, c = here()
     zh = z // 4
     del dense
+    copies = [
+        pltpu.make_async_copy(rand_any, rand, sem.at[0]),
+        pltpu.make_async_copy(glob_any, glob, sem.at[1]),
+    ]
+    for cp in copies:
+        cp.start()
+    for cp in copies:
+        cp.wait()
 
     def add(block, here_too, src, entry):
         bx, bc, bp, bh = place(block)
@@ -648,17 +691,22 @@
     nothing = lambda py, pz: None
     some = [gall.at[pl.ds(0, PLANE - 1), t] for t in range(2)]
     play(
-        reduce_flow(term(0), got_k, out_k, ("z", "y"), pos, c, (k_ssem, k_rsem), finish(0), 32),
-        reduce_flow(term(1), got_v, out_v, ("y", "z"), pos, c, (v_ssem, v_rsem), finish(1), 32),
-        gather_flow(piece(0), half(0), ("y", "z"), pos, c, (o_ssem, o_rsem), nothing, 8, some[0]),
-        gather_flow(piece(1), half(1), ("z", "y"), pos, c, (w_ssem, w_rsem), nothing, 8, some[1]),
+        (
+            reduce_flow(term(0), got_k, out_k, ("z", "y"), pos, c, (k_ssem, k_rsem), finish(0), 32)[0],
+            reduce_flow(term(1), got_v, out_v, ("y", "z"), pos, c, (v_ssem, v_rsem), finish(1), 32)[0],
+            gather_flow(piece(0), half(0), ("y", "z"), pos, c, (o_ssem, o_rsem), nothing, 8, some[0]),
+            gather_flow(piece(1), half(1), ("z", "y"), pos, c, (w_ssem, w_rsem), nothing, 8, some[1]),
+        )
     )
 
 
-def kernel_d(glob, sums, near_sum, att_in, dq_in, gall, att, dq, dk, dv):
+def kernel_d(glob_any, sums, near_sum, att_in, dq_in, gall, att, dq, dk, dv, glob, sem):
+    cp = pltpu.make_async_copy(glob_any, glob, sem.at[0])
+    cp.start()
     shard = lax.axis_index("pb") * 8 + lax.axis_index("ka")
     dk[...] = (sums[0] + near_sum[0]).astype(BF16)
     dv[...] = (sums[1] + near_sum[1]).astype(BF16)
+    cp.wait()
     for j in range(2):
         blocks = jnp.full((16, HD), shard * 2 + j, jnp.int32)
         is_glob = [blocks == glob[g] for g in range(2)]
@@ -667,6 +715,10 @@
                 cols = slice((p // 4) * HD, (p // 4 + 1) * HD)
                 value = jnp.where(is_glob[1], gall[p, t, 1], src[j, p % 4, :, cols])
                 dst[j, p % 4, :, cols] = jnp.where(is_glob[0], gall[p, t, 0], value)
+
+
+def in_hbm(value):
+    return pltpu.with_memory_space_constraint(value, pltpu.HBM)
 
 
 def body(queries, key_vectors, value_vectors, out_grad, rand_blocks, global_blocks):
@@ -696,14 +748,15 @@
         in_specs=[off] * 6,
         out_specs=(vmem, vmem, vmem, vmem, vmem, vmem, hbm),
         scratch_shapes=[
-            pltpu.VMEM((2, PLANE, 2, 2, BLOCK, HD), BF16),
+            pltpu.VMEM((2, PLANE, 2, BLOCK, HD), BF16),
+            pltpu.VMEM((2, PLANE, 2, BLOCK, HD), BF16),
             pltpu.VMEM((PLANE, 64, HD), BF16),
             pltpu.VMEM((mv, 64, HD), BF16),
             pltpu.VMEM((mv, 64, HD), BF16),
             pltpu.VMEM((8, 2, 2, 16, HD), BF16),
-            pltpu.VMEM((2, 2, 4, 2, BLOCK, HD), BF16),
-            pltpu.VMEM((2, 13, 2, BLOCK, HD), BF16),
-            pltpu.VMEM((3, 9, 2, BLOCK, HD), BF16),
+            *[pltpu.VMEM((2, 4, BLOCK, HD), BF16)] * 4,
+            pltpu.VMEM((2, 2, 13, BLOCK, HD), BF16),
+            pltpu.VMEM((2, 3, 9, BLOCK, HD), BF16),
             pltpu.VMEM((8, 32, HD), F32),
             pltpu.VMEM((8, 2, 32, HD), F32),
             pltpu.SMEM((3, 16), jnp.int32),
@@ -723,24 +776,30 @@
             pltpu.VMEM((2, 512, HD), F32),
             pltpu.VMEM((4, HD, HD), F32),
             dma((1,)), dma((ga,)), dma((1,)), dma((gb,)), dma((1,)), dma((mv,)),
-            dma((8,)), dma((8,)), dma((6,)), dma((6,)), dma((12,)), dma((12,)), dma((6,)),
+            dma((8,)), dma((8,)), dma((12,)), dma((12,)), dma((12,)), dma((12,)), dma((6,)),
         ],
         compiler_params=pltpu.CompilerParams(
             collective_id=0, has_side_effects=True, vmem_limit_bytes=VMEM_A
         ),
     )(
-        rand, global_blocks, queries.reshape(rows),
-        key_vectors.reshape(2, BLOCK, HD), value_vectors.reshape(2, BLOCK, HD), out_grad.reshape(rows),
+        *[
+            in_hbm(value)
+            for value in (
+                rand, global_blocks, queries.reshape(rows), key_vectors.reshape(2, BLOCK, HD),
+                value_vectors.reshape(2, BLOCK, HD), out_grad.reshape(rows),
+            )
+        ]
     )
     acc = pl.pallas_call(
         kernel_b,
         name="spread_terms",
         out_shape=shape((PLANE, 2, HD, HD), F32),
-        in_specs=[smem, smem, smem, vmem, vmem],
+        in_specs=[off, smem, off, vmem, vmem],
         out_specs=vmem,
+        scratch_shapes=[pltpu.SMEM((3, 16), jnp.int32), pltpu.SMEM((2,), jnp.int32), dma((2,))],
         input_output_aliases={4: 0},
         compiler_params=pltpu.CompilerParams(vmem_limit_bytes=VMEM_B),
-    )(rand, rand_sib, global_blocks, contrib, dense)
+    )(in_hbm(rand), rand_sib, in_hbm(global_blocks), contrib, dense)
     sums, gall = pl.pallas_call(
         kernel_c,
         name="reduce_and_gather",
@@ -761,10 +820,11 @@
         kernel_d,
         name="finish",
         out_shape=(shape(rows, BF16), shape(rows, BF16), shape((HD, HD), BF16), shape((HD, HD), BF16)),
-        in_specs=[smem] + [vmem] * 5,
+        in_specs=[off] + [vmem] * 5,
         out_specs=(vmem,) * 4,
+        scratch_shapes=[pltpu.SMEM((2,), jnp.int32), dma((1,))],
         compiler_params=pltpu.CompilerParams(vmem_limit_bytes=VMEM_D),
-    )(global_blocks, sums, near_sum, att, dq, gall)
+    )(in_hbm(global_blocks), sums, near_sum, att, dq, gall)
     return att.reshape(queries.shape), dq.reshape(queries.shape), dk, dv
 
 

time: 107 us -> 101 us (0.944)
  local copies, waits for them, and re-layouts: 4.74 us -> 0 us
  Pallas kernels: 101 us -> 99.9 us
    unnamed x12 -> x0, local copies, waits for them, and re-layouts: 4.74 us -> none
    pallas_call x1, Pallas kernels: 29.9 us -> 25.9 us  [body(): pl.pallas_call(kernel_c, name='reduce_and_gather', out_shape=(shape((2, H...]
    pallas_call x1, Pallas kernels: 66 us -> 67.9 us  [body(): pl.pallas_call(kernel_a, name='exchange_and_attend', out_shape=(shape(row...]
where the time goes in v3:
time: 101 us
  Pallas kernels  99.9 us (99%)
    pallas_call x1, Pallas kernels, body(): pl.pallas_call(kernel_a, name='exchange_and_attend', out_shape=(shape(row...  67.9 us
    pallas_call x1, Pallas kernels, body(): pl.pallas_call(kernel_c, name='reduce_and_gather', out_shape=(shape((2, H...  25.9 us
    pallas_call x1, Pallas kernels, body(): pl.pallas_call(kernel_b, name='spread_terms', out_shape=shape((PLANE, 2,...  4.4 us

profile of v3, /device:TPU:2, one launch (start us, length us, event | category | flops | bytes accessed | tf_op | source)
XLA Modules:
  0.0 100.7 jit_solution(11580512510128564789)
XLA Ops:
  0.6 67.9 %exchange_and_attend.1 = (bf16[2,4,16,1024]{3,2,1,0:T(8,128)(2,1)S(1)}, bf16[2,4,16,1024]{3,2,1,0:T(8,128)(2,1)S(1)}, bf16[8,10,2,64,128]{4,3,2,1,0:T(8,128)(2,1...) custom-call(s32[3,16]{1,0:T(4,128)} %bitcast.11, ...), custom_call_target="tpu_custom_call" | custom-call | tf_op jit(solution)/shard_map/exchange_and_attend/pallas_call | solution.py:736
  68.5 4.4 %spread_terms.1.acc = f32[32,2,128,128]{3,2,1,0:T(8,128)S(1)} custom-call(s32[3,16]{1,0:T(4,128)} %bitcast.12, s32[3,16]{1,0:T(4,128)S(1)} %get-tuple-element.17.rand_sib, s32[2]{0:T(128)} %glob_any.5, bf16[8,10,2,64,128]{4,3,2,1,0:T(8,128)(2,1)S(1)} %get-tuple-element.18.contrib, ...), custom_call_target="tpu_custom_call", output_to_operand_aliasing={{}: (4, {})} | custom-call | tf_op jit(solution)/shard_map/spread_terms/pallas_call | solution.py:793
  73.0 25.9 %reduce_and_gather.1 = (f32[2,128,128]{2,1,0:T(8,128)S(1)}, bf16[32,2,2,16,128]{4,3,2,1,0:T(8,128)(2,1)S(1)}) custom-call(f32[32,2,128,128]{3,2,1,0:T(8,128)S(1)} %spread_terms.1.acc, bf16[2,2,16,128]{3,2,1,0:T(8,128)(2,1)S(1)} %get-tuple-element.20.gout), custom_call_target="tpu_custom_call" | custom-call | tf_op jit(solution)/shard_map/reduce_and_gather/pallas_call | solution.py:803
  98.9 1.6 %finish.1 = (bf16[2,4,16,1024]{3,2,1,0:T(8,128)(2,1)}, bf16[2,4,16,1024]{3,2,1,0:T(8,128)(2,1)}, bf16[128,128]{1,0:T(8,128)(2,1)}, bf16[128,128]{1,0:T(8,128)(2,1)}) custom-call(s32[2]{0:T(128)} %glob_any.5, f32[2,128,128]{2,1,0:T(8,128)S(1)} %get-tuple-element.21.sums, f32[2,128,128]{2,1,0:T(8,128)S(1)} %get-tuple-element.22.near_sum, ...), custom_call_target="tpu_custom_call" | custom-call | tf_op jit(solution)/shard_map/finish/pallas_call | solution.py:819

commit v4 on v3

--- a/solution.py
+++ b/solution.py
@@ -43,7 +43,7 @@
     )
 
 
-RATE, CORE_RATE, LATENCY, AHEAD, FAVOUR = 50.0, 200.0, 1.6, 2.0, 0
+RATE, CORE_RATE, LATENCY, AHEAD, FAVOUR = 70.0, 200.0, 1.6, 2.0, 0
 
 
 def schedule(msgs, favoured=()):

time: 101 us -> 99.9 us (0.989)
  Pallas kernels: 99.9 us -> 98.2 us
    pallas_call x1, Pallas kernels: 67.9 us -> 65.5 us  [body(): pl.pallas_call(kernel_a, name='exchange_and_attend', out_shape=(shape(row...]
where the time goes in v4:
time: 99.9 us; the launch traced here: 99 us
  Pallas kernels  98.2 us (98%)
    pallas_call x1, Pallas kernels, body(): pl.pallas_call(kernel_a, name='exchange_and_attend', out_shape=(shape(row...  65.5 us
    pallas_call x1, Pallas kernels, body(): pl.pallas_call(kernel_c, name='reduce_and_gather', out_shape=(shape((2, H...  26.8 us
    pallas_call x1, Pallas kernels, body(): pl.pallas_call(kernel_b, name='spread_terms', out_shape=shape((PLANE, 2,...  4.34 us

profile of v4, /device:TPU:2, one launch (start us, length us, event | category | flops | bytes accessed | tf_op | source)
XLA Modules:
  0.0 99.0 jit_solution(550054027242268023)
XLA Ops:
  0.6 65.5 %exchange_and_attend.1 = (bf16[2,4,16,1024]{3,2,1,0:T(8,128)(2,1)S(1)}, bf16[2,4,16,1024]{3,2,1,0:T(8,128)(2,1)S(1)}, bf16[8,10,2,64,128]{4,3,2,1,0:T(8,128)(2,1...) custom-call(s32[3,16]{1,0:T(4,128)} %bitcast.11, ...), custom_call_target="tpu_custom_call" | custom-call | tf_op jit(solution)/shard_map/exchange_and_attend/pallas_call | solution.py:736
  66.1 4.3 %spread_terms.1.acc = f32[32,2,128,128]{3,2,1,0:T(8,128)S(1)} custom-call(s32[3,16]{1,0:T(4,128)} %bitcast.12, s32[3,16]{1,0:T(4,128)S(1)} %get-tuple-element.17.rand_sib, s32[2]{0:T(128)} %glob_any.5, bf16[8,10,2,64,128]{4,3,2,1,0:T(8,128)(2,1)S(1)} %get-tuple-element.18.contrib, ...), custom_call_target="tpu_custom_call", output_to_operand_aliasing={{}: (4, {})} | custom-call | tf_op jit(solution)/shard_map/spread_terms/pallas_call | solution.py:793
  70.4 26.8 %reduce_and_gather.1 = (f32[2,128,128]{2,1,0:T(8,128)S(1)}, bf16[32,2,2,16,128]{4,3,2,1,0:T(8,128)(2,1)S(1)}) custom-call(f32[32,2,128,128]{3,2,1,0:T(8,128)S(1)} %spread_terms.1.acc, bf16[2,2,16,128]{3,2,1,0:T(8,128)(2,1)S(1)} %get-tuple-element.20.gout), custom_call_target="tpu_custom_call" | custom-call | tf_op jit(solution)/shard_map/reduce_and_gather/pallas_call | solution.py:803
  97.2 1.6 %finish.1 = (bf16[2,4,16,1024]{3,2,1,0:T(8,128)(2,1)}, bf16[2,4,16,1024]{3,2,1,0:T(8,128)(2,1)}, bf16[128,128]{1,0:T(8,128)(2,1)}, bf16[128,128]{1,0:T(8,128)(2,1)}) custom-call(s32[2]{0:T(128)} %glob_any.5, f32[2,128,128]{2,1,0:T(8,128)S(1)} %get-tuple-element.21.sums, f32[2,128,128]{2,1,0:T(8,128)S(1)} %get-tuple-element.22.near_sum, ...), custom_call_target="tpu_custom_call" | custom-call | tf_op jit(solution)/shard_map/finish/pallas_call | solution.py:819

commit v5 on v4

--- a/solution.py
+++ b/solution.py
@@ -43,7 +43,7 @@
     )
 
 
-RATE, CORE_RATE, LATENCY, AHEAD, FAVOUR = 70.0, 200.0, 1.6, 2.0, 0
+RATE, CORE_RATE, LATENCY, AHEAD, FAVOUR = 90.0, 200.0, 1.6, 2.0, 0
 
 
 def schedule(msgs, favoured=()):

time: 99.9 us -> 99.3 us (level)
  no operation moved by 1% of the time
where the time goes in v5:
time: 99.3 us; the launch traced here: 99 us
  Pallas kernels  98.2 us (99%)
    pallas_call x1, Pallas kernels, body(): pl.pallas_call(kernel_a, name='exchange_and_attend', out_shape=(shape(row...  65 us
    pallas_call x1, Pallas kernels, body(): pl.pallas_call(kernel_c, name='reduce_and_gather', out_shape=(shape((2, H...  27.3 us
    pallas_call x1, Pallas kernels, body(): pl.pallas_call(kernel_b, name='spread_terms', out_shape=shape((PLANE, 2,...  4.34 us

profile of v5, /device:TPU:2, one launch (start us, length us, event | category | flops | bytes accessed | tf_op | source)
XLA Modules:
  0.0 99.0 jit_solution(14811716110656873550)
XLA Ops:
  0.6 65.0 %exchange_and_attend.1 = (bf16[2,4,16,1024]{3,2,1,0:T(8,128)(2,1)S(1)}, bf16[2,4,16,1024]{3,2,1,0:T(8,128)(2,1)S(1)}, bf16[8,10,2,64,128]{4,3,2,1,0:T(8,128)(2,1...) custom-call(s32[3,16]{1,0:T(4,128)} %bitcast.11, ...), custom_call_target="tpu_custom_call" | custom-call | tf_op jit(solution)/shard_map/exchange_and_attend/pallas_call | solution.py:736
  65.6 4.3 %spread_terms.1.acc = f32[32,2,128,128]{3,2,1,0:T(8,128)S(1)} custom-call(s32[3,16]{1,0:T(4,128)} %bitcast.12, s32[3,16]{1,0:T(4,128)S(1)} %get-tuple-element.17.rand_sib, s32[2]{0:T(128)} %glob_any.5, bf16[8,10,2,64,128]{4,3,2,1,0:T(8,128)(2,1)S(1)} %get-tuple-element.18.contrib, ...), custom_call_target="tpu_custom_call", output_to_operand_aliasing={{}: (4, {})} | custom-call | tf_op jit(solution)/shard_map/spread_terms/pallas_call | solution.py:793
  70.0 27.3 %reduce_and_gather.1 = (f32[2,128,128]{2,1,0:T(8,128)S(1)}, bf16[32,2,2,16,128]{4,3,2,1,0:T(8,128)(2,1)S(1)}) custom-call(f32[32,2,128,128]{3,2,1,0:T(8,128)S(1)} %spread_terms.1.acc, bf16[2,2,16,128]{3,2,1,0:T(8,128)(2,1)S(1)} %get-tuple-element.20.gout), custom_call_target="tpu_custom_call" | custom-call | tf_op jit(solution)/shard_map/reduce_and_gather/pallas_call | solution.py:803
  97.2 1.6 %finish.1 = (bf16[2,4,16,1024]{3,2,1,0:T(8,128)(2,1)}, bf16[2,4,16,1024]{3,2,1,0:T(8,128)(2,1)}, bf16[128,128]{1,0:T(8,128)(2,1)}, bf16[128,128]{1,0:T(8,128)(2,1)}) custom-call(s32[2]{0:T(128)} %glob_any.5, f32[2,128,128]{2,1,0:T(8,128)S(1)} %get-tuple-element.21.sums, f32[2,128,128]{2,1,0:T(8,128)S(1)} %get-tuple-element.22.near_sum, ...), custom_call_target="tpu_custom_call" | custom-call | tf_op jit(solution)/shard_map/finish/pallas_call | solution.py:819
